TPU v7x, 32 devices: a whole 2x2x4 slice. The times are simulated.
32 devices in a mesh: tm: 8 (over z, x), rows: 4 (over y, core).
Axes of the slice: x: 2, y: 2, z: 4, core: 2. Of those that a mesh axis runs over, the one named last changes fastest.
Arguments:
- slc_stack: bfloat16 [32, 2, 32, 2048], P('tm', None, 'rows'), may hold values from -6 to 6
- partner_count: int32 [32], P('tm'), may hold values from 2 to 6, as said below
- look_sizes: int32 [32, 2], P('tm'), may hold values from 1 to 8, as said below
Outputs:
- interferogram: bfloat16 [32, 6, 2, 32, 2048], P('tm', None, None, 'rows')
- coherence: bfloat16 [32, 6, 32, 2048], P('tm', None, 'rows')
Inputs may be any that keep to these rules, and one draw needn't show every extreme that they name: `partner_count`: some acquisition has 6 partners and some has 2. `look_sizes`: Half-heights run from 1 to 2, half-widths from 2 to 8; some acquisition has (2, 8) and some (1, 2).
All inputs are finite; a program needn't handle non-finite values.
Results may differ from a plain program's by a relative error of at most 0.0049.
Values may be sent and summed in bfloat16 or wider, within the bound.
A program may use at most 64 MiB of HBM per device.

v0:
```python
import jax
import jax.numpy as jnp
import numpy as np
from jax import lax
from jax.sharding import PartitionSpec as P

MAXP = 6
HR = 2


epsilon = 1e-06


def extended_2(block, sides, width):
    for axis, dim in sides:
        count = lax.axis_size(axis)
        forward = [(i, i + 1) for i in range(count - 1)]
        backward = [(target, source) for source, target in forward]
        low = lax.ppermute(
            lax.slice_in_dim(block, block.shape[dim] - width, None, axis=dim), axis, forward
        )
        high = lax.ppermute(lax.slice_in_dim(block, 0, width, axis=dim), axis, backward)
        block = jnp.concatenate([low, block, high], axis=dim)
    return block


def passed_along(block, axis, distance):
    devices = range(lax.axis_size(axis))
    route = [(i - distance, i) for i in devices if i - distance in devices]
    return lax.ppermute(block, axis, route)


def window_rows(fields, half_rows):
    row_count = fields.shape[-2] - 2 * HR
    shape_tail = (1,) * (fields.ndim - 1)
    total = jnp.zeros(fields.shape[:-2] + (row_count, fields.shape[-1]), jnp.float32)
    for offset in range(-HR, HR + 1):
        weight = (
            (jnp.abs(offset) <= half_rows)
            .astype(jnp.float32)
            .reshape((fields.shape[0],) + shape_tail)
        )
        total = total + weight * fields[..., HR + offset : HR + offset + row_count, :]
    return total


def make_bands(half_cols):
    inner = jnp.arange(384, dtype=jnp.int32)
    outer = jnp.arange(256, dtype=jnp.int32)
    distance = jnp.abs(inner[:, None] - 64 - outer[None, :])
    band = (distance[None] <= half_cols[:, None, None]).astype(jnp.bfloat16)
    return (band[:, :256], band[:, 256:])


def window_cols(summed, band_lead, band_tail):
    col_count = summed.shape[-1]
    blocks = col_count // 256
    padded = jnp.pad(summed, [(0, 0)] * (summed.ndim - 1) + [(64, 192)])
    lead_part = padded[..., :col_count].reshape(summed.shape[:-1] + (blocks, 256))
    tail_part = padded[..., 256 : col_count + 256].reshape(summed.shape[:-1] + (blocks, 256))[
        ..., :128
    ]
    result = jnp.einsum(
        "p...i,pij->p...j", lead_part, band_lead, preferred_element_type=jnp.float32
    )
    result = result + jnp.einsum(
        "p...i,pij->p...j", tail_part, band_tail, preferred_element_type=jnp.float32
    )
    return result.reshape(summed.shape)


def slot_fields(own_data, partners, half_rows, band_lead, band_tail, boxed_own, area):
    partner_data = partners.astype(jnp.float32)
    real_part = (
        own_data[:, :, 0] * partner_data[:, :, 0] + own_data[:, :, 1] * partner_data[:, :, 1]
    )
    imag_part = (
        own_data[:, :, 1] * partner_data[:, :, 0] - own_data[:, :, 0] * partner_data[:, :, 1]
    )
    power = (
        partner_data[:, :, 0] * partner_data[:, :, 0]
        + partner_data[:, :, 1] * partner_data[:, :, 1]
    )
    terms = jnp.stack([real_part, imag_part, power], 2)
    boxed = window_cols(window_rows(terms, half_rows).astype(jnp.bfloat16), band_lead, band_tail)
    ifg = boxed[:, :, :2] / area[:, None, None, None, None]
    magnitude = jnp.sqrt(boxed[:, :, 0] * boxed[:, :, 0] + boxed[:, :, 1] * boxed[:, :, 1])
    coh = magnitude * lax.rsqrt(boxed_own * boxed[:, :, 2] + epsilon)
    return (ifg, coh)


def local(slc_stack, partner_count, look_sizes):
    per_dev = slc_stack.shape[0]
    haloed = extended_2(slc_stack, (("rows", 2),), HR)
    nearby = passed_along(haloed, "tm", -1)
    farther = passed_along(haloed[: MAXP - per_dev], "tm", -2)
    extended = jnp.concatenate([haloed, nearby, farther], 0)
    half_rows = look_sizes[:, 0]
    half_cols = look_sizes[:, 1]
    band_lead, band_tail = make_bands(half_cols)
    area = ((2 * half_rows + 1) * (2 * half_cols + 1)).astype(jnp.float32)
    own_data = haloed.astype(jnp.float32)
    own_power = (own_data[:, 0] * own_data[:, 0] + own_data[:, 1] * own_data[:, 1])[:, None]
    boxed_own = window_cols(
        window_rows(own_power, half_rows).astype(jnp.bfloat16), band_lead, band_tail
    )
    acq_total = lax.axis_size("tm") * per_dev
    global_index = lax.axis_index("tm") * per_dev + jnp.arange(per_dev, dtype=jnp.int32)
    offsets = jnp.arange(1, MAXP + 1, dtype=jnp.int32)
    static_index = (np.arange(per_dev)[:, None] + np.arange(1, MAXP + 1)[None, :]).reshape(-1)
    partners = extended[static_index].reshape((per_dev, MAXP) + extended.shape[1:])
    ifg, coh = slot_fields(
        own_data[:, None], partners, half_rows, band_lead, band_tail, boxed_own, area
    )
    live = (offsets[None, :] <= partner_count[:, None]) & (
        global_index[:, None] + offsets[None, :] < acq_total
    )
    interferogram = jnp.where(live[:, :, None, None, None], ifg, 0.0).astype(jnp.bfloat16)
    coherence = jnp.where(live[:, :, None, None], coh, 0.0).astype(jnp.bfloat16)
    return (interferogram, coherence)


def solution(mesh):
    return jax.shard_map(
        local,
        mesh=mesh,
        in_specs=(P("tm", None, "rows", None), P("tm"), P("tm", None)),
        out_specs=(P("tm", None, None, "rows", None), P("tm", None, "rows", None)),
        check_vma=False,
    )
```

profile of v0, /device:TPU:1, one launch (start us, length us, event | category | flops | bytes accessed | tf_op | source)
XLA Modules:
  0.0 72.6 jit_solution(5583667450524623500)
XLA Ops:
  0.6 0.0 copy-start.1
  0.6 1.2 %fusion.43 = (bf16[4,2,2,2048]{3,2,1,0:T(2,128)(2,1)S(1)}, bf16[4,2,2,2048]{3,2,1,0:T(2,128)(2,1)S(1)}) fusion(bf16[4,2,8,2048]{3,2,1,0:T(8,128)(2,1)} %param.5), kind=kLoop, calls=%fused_computation.89 | loop fusion | bytes 262144 | tf_op jit(solution)/shard_map/slice | solution.py:20
  1.8 4.5 %collective-permute-start = (bf16[4,2,2,2048]{3,2,1,0:T(2,128)(2,1)S(1)}, bf16[4,2,2,2048]{3,2,1,0:T(2,128)(2,1)S(1)}, u32[]{:S(2)}, u32[]{:S(2)}) collective-permute-start(bf16[4,2,2,2048]{3,2,1,0:T(2,128)(2,1)S(1)} %get-tuple-element.11), channel_id=1, source_target_pairs={{0,1},{1,2},{2,3},{4,5},{5,6},{6,7},{8,9},{9,10},{10,11},{12,13},{... | collective-permute-start | bytes 196616 | tf_op jit(solution)/shard_map/ppermute | solution.py:19
  6.4 1.9 %collective-permute-start.1 = (bf16[4,2,2,2048]{3,2,1,0:T(2,128)(2,1)S(1)}, bf16[4,2,2,2048]{3,2,1,0:T(2,128)(2,1)S(1)}, u32[]{:S(2)}, u32[]{:S(2)}) collective-permute-start(bf16[4,2,2,2048]{3,2,1,0:T(2,128)(2,1)S(1)} %get-tuple-element.12), channel_id=1, source_target_pairs={{1,0},{2,1},{3,2},{5,4},{6,5},{7,6},{9,8},{10,9},{11,10},{13,12},{... | collective-permute-start | bytes 196616 | tf_op jit(solution)/shard_map/ppermute | solution.py:22
  8.3 0.8 %fusion.41 = f32[4]{0:T(128)S(1)} fusion(s32[4,2]{0,1:T(2,128)} %param.7), kind=kLoop, calls=%fused_computation.84 | loop fusion | flops 24 | bytes 48 | tf_op jit(solution)/shard_map/convert_element_type | solution.py:101
  9.1 0.7 slice_bitcast_fusion.7
  9.8 0.7 fusion.38
  10.4 0.1 subtract_abs_fusion
  10.6 0.3 broadcast_compare_fusion
  10.8 0.7 %fusion.37 = pred[4,6]{1,0:T(4,128)(4,1)S(1)} fusion(s32[4]{0:T(128)S(1)} %iota_add_fusion.1, s32[6]{0:T(128)S(1)} %iota_add_fusion.2, s32[4]{0:T(128)} %param.6), kind=kLoop, calls=%fused_computation.76 | loop fusion | flops 96 | bytes 80 | tf_op jit(solution)/shard_map/and | solution.py:115
  11.6 0.7 pad_clamp_fusion
  12.2 0.0 collective-permute-done
  12.2 0.0 collective-permute-done.1
  12.2 1.2 %fusion.42 = (f32[4,2,12,2048]{3,2,1,0:T(8,128)S(1)}, bf16[4,2,12,2048]{3,2,1,0:T(8,128)(2,1)S(1)}) fusion(bf16[4,2,2,2048]{3,2,1,0:T(2,128)(2,1)S(1)} %collective-permute-done.1, bf16[4,2,8,2048]{3,2,1,0:T(8,128)(2,1)} %param.5, bf16[4,2,2,2048]{3,2,1,0:T(2,128)(2,1)S(1)} %collective-permute-done), kind=kLoop, calls=%fused_computation.88 | loop fusion | flops 1376256 | bytes 1572864 | tf_op jit(solution)/shard_map/convert_element_type | solution.py:102
  13.5 1.3 %collective-permute-start.2 = (bf16[4,2,12,2048]{3,2,1,0:T(8,128)(2,1)S(1)}, bf16[4,2,12,2048]{3,2,1,0:T(8,128)(2,1)}, u32[]{:S(2)}, u32[]{:S(2)}) collective-permute-start(bf16[4,2,12,2048]{3,2,1,0:T(8,128)(2,1)S(1)} %get-tuple-element.10), channel_id=1, source_target_pairs={{4,0},{8,4},{12,8},{16,12},{20,16},{24,20},{28,24},{5,1},{9,5},{13... | collective-permute-start | bytes 1179656 | tf_op jit(solution)/shard_map/ppermute | solution.py:30
  14.8 0.0 copy-done.1
  14.8 0.2 maximum_convert_fusion
  15.0 0.1 slice_bitcast_fusion.4
  15.1 0.1 fusion.25
  15.2 0.2 fusion.31
  15.4 0.1 pad_slice_fusion.2
  15.5 1.3 %collective-permute-start.3 = (bf16[2,2,12,2048]{3,2,1,0:T(8,128)(2,1)S(1)}, bf16[2,2,12,2048]{3,2,1,0:T(8,128)(2,1)S(1)}, u32[]{:S(2)}, u32[]{:S(2)}) collective-permute-start(bf16[2,2,12,2048]{3,2,1,0:T(8,128)(2,1)S(1)} %slice.147), channel_id=1, source_target_pairs={{8,0},{12,4},{16,8},{20,12},{24,16},{28,20},{9,1},{13,5},{17,9},{2... | collective-permute-start | bytes 589832 | tf_op jit(solution)/shard_map/ppermute | solution.py:30
  16.8 0.3 fusion.20
  17.1 0.2 convolution_add_fusion.1
  17.3 0.7 %mul.204 = f32[4,8,2048]{2,1,0:T(8,128)} reshape(f32[4,8,8,256]{3,2,1,0:T(8,128)S(1)} %convolution_add_fusion.1) | data formatting | bytes 524288 | tf_op jit(solution)/shard_map/mul | solution.py:88
  18.1 16.0 %collective-permute-done.3 = bf16[2,2,12,2048]{3,2,1,0:T(8,128)(2,1)S(1)} collective-permute-done((bf16[2,2,12,2048]{3,2,1,0:T(8,128)(2,1)S(1)}, bf16[2,2,12,2048]{3,2,1,0:T(8,128)(2,1)S(1)}, u32[]{:S(2)}, u32[]{:S(2)}) %collective-permute-start.3) | collective-permute-done | bytes 196640 | tf_op jit(solution)/shard_map/ppermute | solution.py:30
  34.1 0.0 copy-start.3
  34.1 0.7 copy-done.3
  34.8 0.0 collective-permute-done.2
  34.8 1.4 %pad_maximum_fusion.1 = bf16[10,2,12,2048]{3,2,1,0:T(8,128)(2,1)S(1)} fusion(bf16[2,2,12,2048]{3,2,1,0:T(8,128)(2,1)} %copy-done.3, bf16[4,2,12,2048]{3,2,1,0:T(8,128)(2,1)} %collective-permute-done.2, bf16[4,2,2,2048]{3,2,1,0:T(2,128)(2,1)S(1)} %collective-permute-done.1, bf16[4,2,8,2048]{3,2,1,0:T(8,128)(2,1)S(1)} %copy-done.1, ...), kind=kLoop, calls=%fused_computation.35 | loop fusion | flops 4915200 | bytes 1966080 | tf_op jit(solution)/shard_map/concatenate | solution.py:97
  36.3 2.5 %gather_fusion = bf16[24,2,12,2048]{3,2,1,0:T(8,128)(2,1)} fusion(bf16[10,2,12,2048]{3,2,1,0:T(8,128)(2,1)S(1)} %pad_maximum_fusion.1, s32[1024]{0:T(1024)S(1)} %pad_clamp_fusion), kind=kCustom, calls=%fused_computation | custom fusion | bytes 4718688 | tf_op jit(solution)/shard_map/gather | solution.py:111
  38.7 2.7 %convert.4 = f32[4,6,2,12,2048]{4,3,2,1,0:T(8,128)S(1)} convert(bf16[4,6,2,12,2048]{4,3,2,1,0:T(8,128)(2,1)} %bitcast.115) | non-fusion elementwise | flops 1179648 | bytes 7077888 | tf_op jit(solution)/shard_map/convert_element_type | solution.py:73
  41.5 3.1 %multiply_add_fusion.1 = (f32[4,6,1,12,2048]{4,3,2,1,0:T(8,128)S(1)}, f32[4,6,1,12,2048]{4,3,2,1,0:T(8,128)S(1)}, f32[4,6,1,12,2048]{4,3,2,1,0:T(8,128)}) fusion(f32[4,6,2,12,2048]{4,3,2,1,0:T(8,128)S(1)} %convert.4, f32[4,12,2048]{2,1,0:T(8,128)S(1)} %get-tuple-element.8, f32[4,12,2048]{2,1,0:T(8,128)S(1)} %get-tuple-element.7), kind=kLoop, calls=%fused_computation.17 | loop fusion | flops 5308416 | bytes 12582912 | tf_op jit(solution)/shard_map/add | solution.py:75
  44.6 2.3 %pad_maximum_fusion = f32[4,6,3,12,2048]{4,3,2,1,0:T(8,128)S(1)} fusion(f32[4,6,1,12,2048]{4,3,2,1,0:T(8,128)} %get-tuple-element.4, f32[4,6,1,12,2048]{4,3,2,1,0:T(8,128)S(1)} %get-tuple-element.3, f32[4,6,1,12,2048]{4,3,2,1,0:T(8,128)S(1)} %get-tuple-element.2), kind=kLoop, calls=%fused_computation.1 | loop fusion | flops 3538944 | bytes 14155776 | tf_op jit(solution)/shard_map/stack | solution.py:84
  46.9 3.8 %fusion.1 = bf16[4,6,3,8,2048]{4,3,2,1,0:T(8,128)(2,1)} fusion(f32[4,6,3,12,2048]{4,3,2,1,0:T(8,128)S(1)} %pad_maximum_fusion, f32[4]{0:T(128)S(1)} %get-tuple-element.17, f32[4]{0:T(128)S(1)} %get-tuple-element.16, f32[4]{0:T(128)S(1)} %get-tuple-element.15), kind=kLoop, calls=%fused_computation.4 | loop fusion | flops 11796480 | bytes 25952304 | tf_op jit(solution)/shard_map/convert_element_type | solution.py:85
  50.7 4.7 %pad_slice_fusion.1 = (bf16[4,6,3,8,2048]{4,3,2,1,0:T(8,128)(2,1)S(1)}, bf16[4,6,3,8,2048]{4,3,2,1,0:T(8,128)(2,1)S(1)}) fusion(bf16[4,6,3,8,2048]{4,3,2,1,0:T(8,128)(2,1)} %fusion.1), kind=kLoop, calls=%fused_computation.19 | loop fusion | bytes 7077888 | tf_op jit(solution)/shard_map/slice | solution.py:59
  55.4 0.8 %copy.17 = bf16[72,8,8,256]{3,2,1,0:T(8,128)(2,1)S(1)} copy(bf16[72,8,8,256]{3,1,2,0:T(8,128)(2,1)S(1)} %bitcast.117) | data formatting | bytes 4718592
  56.2 0.8 %copy.18 = bf16[72,8,8,256]{3,2,1,0:T(8,128)(2,1)S(1)} copy(bf16[72,8,8,256]{3,1,2,0:T(8,128)(2,1)S(1)} %bitcast.116) | data formatting | bytes 4718592
  57.0 0.8 %fusion.18 = f32[4,6,3,8,8,256]{5,4,3,2,1,0:T(8,128)S(1)} fusion(bf16[4,6,3,8,8,256]{5,4,3,2,1,0:T(8,128)(2,1)S(1)} %bitcast.118, pred[4,384,256]{2,1,0:T(32,128)(4,1)S(1)} %broadcast_compare_fusion), kind=kOutput, calls=%fused_computation.36 | convolution fusion | flops 301989888 | bytes 6029312 | tf_op jit(solution)/shard_map/p...i,pij->p...j/dot_general | solution.py:66
  57.8 3.0 %convolution_add_fusion = f32[4,6,3,8,8,256]{5,4,3,2,1,0:T(8,128)} fusion(f32[4,6,3,8,8,256]{5,4,3,2,1,0:T(8,128)S(1)} %fusion.18, bf16[4,6,3,8,8,256]{5,4,3,2,1,0:T(8,128)(2,1)S(1)} %bitcast.114, pred[4,384,256]{2,1,0:T(32,128)(4,1)S(1)} %broadcast_compare_fusion), kind=kOutput, calls=%fused_computation.20 | convolution fusion | flops 605159424 | bytes 12058624 | tf_op jit(solution)/shard_map/p...i,pij->p...j/dot_general | solution.py:63
  60.8 0.0 copy-start.2
  60.8 6.0 %reshape.311 = f32[4,6,3,8,2048]{4,3,2,1,0:T(8,128)} reshape(f32[4,6,3,8,8,256]{5,4,3,2,1,0:T(8,128)} %convolution_add_fusion) | data formatting | bytes 9437184 | tf_op jit(solution)/shard_map/reshape | solution.py:69
  66.8 0.0 copy-done.2
  66.8 0.0 copy-start
  66.8 4.2 %fusion.12 = bf16[4,6,8,2048]{3,2,1,0:T(8,128)(2,1)} fusion(f32[4,6,3,8,2048]{4,3,2,1,0:T(8,128)} %reshape.311, f32[4,8,2048]{2,1,0:T(8,128)S(1)} %copy-done.2, pred[4,6]{1,0:T(4,128)(4,1)S(1)} %fusion.37), kind=kLoop, calls=%fused_computation.27 | loop fusion | flops 3145728 | bytes 5767192 | tf_op jit(solution)/shard_map/convert_element_type | solution.py:119
  71.0 0.0 copy-done
  71.0 1.6 %fusion.6 = bf16[4,6,2,8,2048]{4,3,2,1,0:T(8,128)(2,1)} fusion(f32[4,6,3,8,2048]{4,3,2,1,0:T(8,128)S(1)} %copy-done, f32[4]{0:T(128)S(1)} %fusion.41, pred[4,6]{1,0:T(4,128)(4,1)S(1)} %fusion.37), kind=kLoop, calls=%fused_computation.14 | loop fusion | flops 2359296 | bytes 4718632 | tf_op jit(solution)/shard_map/convert_element_type | solution.py:118
  (5 shorter events, 0.1 us)
Async XLA Ops:
  0.6 14.1 %copy-start.1 = (bf16[4,2,8,2048]{3,2,1,0:T(8,128)(2,1)S(1)}, bf16[4,2,8,2048]{3,2,1,0:T(8,128)(2,1)}, u32[]{:S(2)}) copy-start(bf16[4,2,8,2048]{3,2,1,0:T(8,128)(2,1)} %param.5) | copy-start | bytes 786436
  1.8 10.4 %collective-permute-start = (bf16[4,2,2,2048]{3,2,1,0:T(2,128)(2,1)S(1)}, bf16[4,2,2,2048]{3,2,1,0:T(2,128)(2,1)S(1)}, u32[]{:S(2)}, u32[]{:S(2)}) collective-permute-start(bf16[4,2,2,2048]{3,2,1,0:T(2,128)(2,1)S(1)} %get-tuple-element.11), channel_id=1, source_target_pairs={{0,1},{1,2},{2,3},{4,5},{5,6},{6,7},{8,9},{9,10},{10,11},{12,13},{... | collective-permute-start | bytes 196616 | tf_op jit(solution)/shard_map/ppermute | solution.py:19
  6.4 5.9 %collective-permute-start.1 = (bf16[4,2,2,2048]{3,2,1,0:T(2,128)(2,1)S(1)}, bf16[4,2,2,2048]{3,2,1,0:T(2,128)(2,1)S(1)}, u32[]{:S(2)}, u32[]{:S(2)}) collective-permute-start(bf16[4,2,2,2048]{3,2,1,0:T(2,128)(2,1)S(1)} %get-tuple-element.12), channel_id=1, source_target_pairs={{1,0},{2,1},{3,2},{5,4},{6,5},{7,6},{9,8},{10,9},{11,10},{13,12},{... | collective-permute-start | bytes 196616 | tf_op jit(solution)/shard_map/ppermute | solution.py:22
  13.5 21.3 %collective-permute-start.2 = (bf16[4,2,12,2048]{3,2,1,0:T(8,128)(2,1)S(1)}, bf16[4,2,12,2048]{3,2,1,0:T(8,128)(2,1)}, u32[]{:S(2)}, u32[]{:S(2)}) collective-permute-start(bf16[4,2,12,2048]{3,2,1,0:T(8,128)(2,1)S(1)} %get-tuple-element.10), channel_id=1, source_target_pairs={{4,0},{8,4},{12,8},{16,12},{20,16},{24,20},{28,24},{5,1},{9,5},{13... | collective-permute-start | bytes 1179656 | tf_op jit(solution)/shard_map/ppermute | solution.py:30
  15.5 18.6 %collective-permute-start.3 = (bf16[2,2,12,2048]{3,2,1,0:T(8,128)(2,1)S(1)}, bf16[2,2,12,2048]{3,2,1,0:T(8,128)(2,1)S(1)}, u32[]{:S(2)}, u32[]{:S(2)}) collective-permute-start(bf16[2,2,12,2048]{3,2,1,0:T(8,128)(2,1)S(1)} %slice.147), channel_id=1, source_target_pairs={{8,0},{12,4},{16,8},{20,12},{24,16},{28,20},{9,1},{13,5},{17,9},{2... | collective-permute-start | bytes 589832 | tf_op jit(solution)/shard_map/ppermute | solution.py:30
  34.1 0.7 copy-start.3
  60.8 6.0 %copy-start.2 = (f32[4,8,2048]{2,1,0:T(8,128)S(1)}, f32[4,8,2048]{2,1,0:T(8,128)}, u32[]{:S(2)}) copy-start(f32[4,8,2048]{2,1,0:T(8,128)} %mul.204) | copy-start | bytes 786436
  66.8 4.2 %copy-start = (f32[4,6,3,8,2048]{4,3,2,1,0:T(8,128)S(1)}, f32[4,6,3,8,2048]{4,3,2,1,0:T(8,128)}, u32[]{:S(2)}) copy-start(f32[4,6,3,8,2048]{4,3,2,1,0:T(8,128)} %reshape.311) | copy-start | bytes 14155780
where the time goes:
time: 73.1 us; the launch traced here: 72.6 us
  other arithmetic  24.1 us (33%)
  local copies, waits for them, and re-layouts  18.3 us (25%)
  waiting for transfers between devices  16 us (22%)
  starting transfers between devices  9.03 us (12%)
  matrix products  4.28 us (6%)
  between operations  0.83 us (1%)
    ppermute x2, waiting for transfers between devices, passed_along(): return lax.ppermute(block, axis, route)  16 us
    reshape x1, local copies, waits for them, and re-layouts, window_cols(): return result.reshape(summed.shape)  6.01 us
    slice x1, local copies, waits for them, and re-layouts, window_cols(): padded[..., :col_count].reshape(summed.shape[:-1] + (blocks, 256))  4.71 us
    ppermute x1, starting transfers between devices, extended_2(): lax.ppermute(lax.slice_in_dim(block, block.shape[dim] - width, None, axis...  4.53 us
    convert_element_type x1, other arithmetic, local(): coherence = jnp.where(live[:, :, None, None], coh, 0.0).astype(jnp.bfloat16)  4.2 us
    convert_element_type x1, other arithmetic, slot_fields(): window_rows(terms, half_rows).astype(jnp.bfloat16)  3.8 us
    dot_general x2, matrix products, window_cols(): jnp.einsum('p...i,pij->p...j', lead_part, band_lead, preferred_element_ty...  3.26 us
    add x1, other arithmetic, slot_fields(): own_data[:, :, 0] * partner_data[:, :, 0]  3.11 us
  transfers between devices with their start and end apart: 4, of which 1 were waited for; matrix products, arithmetic and copies ran while one was open for 8% of the time, Pallas kernels for 0%

commit v1 on v0

v1 whole, which is shorter than its diff:
```python
import functools

import jax
import jax.numpy as jnp
from jax import lax
from jax.experimental import pallas as pl
from jax.experimental.pallas import tpu as pltpu
from jax.sharding import PartitionSpec as P

MAXP = 6
HR = 2
LANES = 128
BLOCK = 256

epsilon = 1e-06


def extended_2(block, sides, width):
    for axis, dim in sides:
        count = lax.axis_size(axis)
        forward = [(i, i + 1) for i in range(count - 1)]
        backward = [(target, source) for source, target in forward]
        low = lax.ppermute(
            lax.slice_in_dim(block, block.shape[dim] - width, None, axis=dim), axis, forward
        )
        high = lax.ppermute(lax.slice_in_dim(block, 0, width, axis=dim), axis, backward)
        block = jnp.concatenate([low, block, high], axis=dim)
    return block


def passed_along(block, axis, distance):
    devices = range(lax.axis_size(axis))
    route = [(i - distance, i) for i in devices if i - distance in devices]
    return lax.ppermute(block, axis, route)


def compute_kernel(
    acq_total, counts, looks, src, ifg, coh, planes, power, sums, wide, boxed, stage
):
    acq = pl.program_id(0)
    total, _, ext_rows, cols = src.shape
    per_dev = total - MAXP
    rows = ext_rows - 2 * HR
    tiles = cols // LANES
    blocks = cols // BLOCK
    fields = 3 * MAXP + 1

    @pl.when(acq == 0)
    def _():
        @pl.loop(0, total)
        def _(p):
            for part in range(2):
                for t in range(tiles):
                    piece = src[p, part, :, t * LANES : (t + 1) * LANES].astype(jnp.float32)
                    stage[part, t * 16 : t * 16 + ext_rows, :] = piece
            for r in range(ext_rows):
                real = stage[0, pl.ds(r, tiles, stride=16), :]
                imag = stage[1, pl.ds(r, tiles, stride=16), :]
                planes[p, 0, r] = real
                planes[p, 1, r] = imag
                power[p, r] = real * real + imag * imag

        zero = jnp.zeros((wide.shape[1], LANES), wide.dtype)
        wide[0, :, :LANES] = zero
        wide[blocks, :, LANES:] = zero

    half_rows = looks[acq, 0]
    half_cols = looks[acq, 1]
    outer = jnp.where(half_rows >= HR, 1.0, 0.0).astype(jnp.float32)

    def row_window(get, field):
        for h in range(0, tiles, 8):
            x = get(h)
            pairs = [x[r] + x[r + 1] for r in range(1, rows + 2)]
            for r in range(rows):
                inner = pairs[r] + x[r + 3]
                edge = (x[r] + x[r + 4]) * outer
                sums[field, pl.ds(h * rows + r, 8, stride=rows), :] = inner + edge

    def row(p, part, r, h):
        return planes[p, part, r, h : h + 8, :]

    def own_power(h):
        return [power[acq, r, h : h + 8, :] for r in range(ext_rows)]

    row_window(own_power, 3 * MAXP)

    @pl.loop(0, MAXP)
    def _(j):
        p = acq + j + 1

        def real_part(h):
            return [
                row(acq, 0, r, h) * row(p, 0, r, h) + row(acq, 1, r, h) * row(p, 1, r, h)
                for r in range(ext_rows)
            ]

        def imag_part(h):
            return [
                row(acq, 1, r, h) * row(p, 0, r, h) - row(acq, 0, r, h) * row(p, 1, r, h)
                for r in range(ext_rows)
            ]

        def partner_power(h):
            return [power[p, r, h : h + 8, :] for r in range(ext_rows)]

        row_window(real_part, 3 * j)
        row_window(imag_part, 3 * j + 1)
        row_window(partner_power, 3 * j + 2)

    @pl.loop(0, (fields + 1) // 2)
    def _(f):
        for t in range(tiles):
            both = jnp.concatenate(
                [
                    sums[2 * f, t * rows : (t + 1) * rows, :],
                    sums[2 * f + 1, t * rows : (t + 1) * rows, :],
                ],
                0,
            ).astype(jnp.bfloat16)
            m, side = (t + 1) // 2, (t + 1) % 2
            wide[m, pl.ds(pl.multiple_of(f * 16, 16), 16), side * LANES : (side + 1) * LANES] = both

    inner = lax.broadcasted_iota(jnp.int32, (BLOCK, BLOCK), 0)
    place = lax.broadcasted_iota(jnp.int32, (BLOCK, BLOCK), 1)
    lead = jnp.where(jnp.abs(inner - LANES - place) <= half_cols, 1.0, 0.0).astype(jnp.bfloat16)
    tail = jnp.where(jnp.abs(inner + LANES - place) <= half_cols, 1.0, 0.0).astype(jnp.bfloat16)
    depth = wide.shape[1]
    boxed[...] = (
        jnp.dot(
            wide[0:blocks].reshape(blocks * depth, BLOCK), lead, preferred_element_type=jnp.float32
        )
        + jnp.dot(
            wide[1 : blocks + 1].reshape(blocks * depth, BLOCK),
            tail,
            preferred_element_type=jnp.float32,
        )
    ).reshape(blocks, depth, BLOCK)

    area = ((2 * half_rows + 1) * (2 * half_cols + 1)).astype(jnp.float32)
    scale = 1.0 / jnp.full((rows, BLOCK), area, jnp.float32)
    index = lax.axis_index("tm") * per_dev + acq
    count = counts[acq]

    @pl.loop(0, blocks)
    def _(n):
        own = boxed[n, 3 * MAXP * rows : (3 * MAXP + 1) * rows, :]
        where = pl.ds(pl.multiple_of(n * BLOCK, BLOCK), BLOCK)
        for j in range(MAXP):
            live = (j < count) & (index + j + 1 < acq_total)
            real = boxed[n, (3 * j) * rows : (3 * j + 1) * rows, :]
            imag = boxed[n, (3 * j + 1) * rows : (3 * j + 2) * rows, :]
            other = boxed[n, (3 * j + 2) * rows : (3 * j + 3) * rows, :]
            magnitude = jnp.sqrt(real * real + imag * imag)
            value = magnitude * lax.rsqrt(own * other + epsilon)
            ifg[0, j, 0, :, where] = jnp.where(live, real * scale, 0.0).astype(ifg.dtype)
            ifg[0, j, 1, :, where] = jnp.where(live, imag * scale, 0.0).astype(ifg.dtype)
            coh[0, j, :, where] = jnp.where(live, value, 0.0).astype(coh.dtype)


def computed(extended, partner_count, look_sizes, acq_total):
    total, _, ext_rows, cols = extended.shape
    per_dev, rows = total - MAXP, ext_rows - 2 * HR
    tiles, blocks = cols // LANES, cols // BLOCK
    fields = 3 * MAXP + 2
    return pl.pallas_call(
        functools.partial(compute_kernel, acq_total),
        grid=(per_dev,),
        in_specs=[
            pl.BlockSpec(memory_space=pltpu.SMEM),
            pl.BlockSpec(memory_space=pltpu.SMEM),
            pl.BlockSpec(extended.shape, lambda a: (0, 0, 0, 0)),
        ],
        out_specs=[
            pl.BlockSpec((1, MAXP, 2, rows, cols), lambda a: (a, 0, 0, 0, 0)),
            pl.BlockSpec((1, MAXP, rows, cols), lambda a: (a, 0, 0, 0)),
        ],
        out_shape=[
            jax.ShapeDtypeStruct((per_dev, MAXP, 2, rows, cols), jnp.bfloat16),
            jax.ShapeDtypeStruct((per_dev, MAXP, rows, cols), jnp.bfloat16),
        ],
        scratch_shapes=[
            pltpu.VMEM((total, 2, ext_rows, tiles, LANES), jnp.float32),
            pltpu.VMEM((total, ext_rows, tiles, LANES), jnp.float32),
            pltpu.VMEM((fields, tiles * rows, LANES), jnp.float32),
            pltpu.VMEM((blocks + 1, fields * rows, BLOCK), jnp.bfloat16),
            pltpu.VMEM((blocks, fields * rows, BLOCK), jnp.float32),
            pltpu.VMEM((2, tiles * 16, LANES), jnp.float32),
        ],
        compiler_params=pltpu.CompilerParams(vmem_limit_bytes=48 * 1024 * 1024),
        name="insar_boxes",
    )(partner_count, look_sizes, extended)


def local(slc_stack, partner_count, look_sizes):
    per_dev = slc_stack.shape[0]
    haloed = extended_2(slc_stack, (("rows", 2),), HR)
    nearby = passed_along(haloed, "tm", -1)
    farther = passed_along(haloed[: MAXP - per_dev], "tm", -2)
    extended = jnp.concatenate([haloed, nearby, farther], 0)
    acq_total = lax.axis_size("tm") * per_dev
    return tuple(computed(extended, partner_count, look_sizes, acq_total))


def solution(mesh):
    return jax.shard_map(
        local,
        mesh=mesh,
        in_specs=(P("tm", None, "rows", None), P("tm"), P("tm", None)),
        out_specs=(P("tm", None, None, "rows", None), P("tm", None, "rows", None)),
        check_vma=False,
    )
```

time: 73.1 us -> 42 us (0.57)
  other arithmetic: 24.1 us -> 1.52 us
  local copies, waits for them, and re-layouts: 18.3 us -> 1.31 us
  Pallas kernels: 0 us -> 8.1 us
  waiting for transfers between devices: 16 us -> 21 us
  matrix products: 4.28 us -> 0 us
    convert_element_type x9 -> x0, other arithmetic: 15.4 us -> none  [the longest x1 4.2 us: local(): coherence = jnp.where(live[:, :, None, None], coh, 0.0).astype(jnp.bfloat16)]
    pallas_call x0 -> x1, Pallas kernels: none -> 8.1 us  [computed(): pl.pallas_call(functools.partial(compute_kernel, acq_total), grid=(per_de...]
    reshape x1 -> x0, local copies, waits for them, and re-layouts: 6.01 us -> none  [window_cols(): return result.reshape(summed.shape)]
    slice x2 -> x0, local copies, waits for them, and re-layouts: 4.85 us -> none  [the longest x1 4.71 us: window_cols(): padded[..., :col_count].reshape(summed.shape[:-1] + (blocks, 256))]
    dot_general x4 -> x0, matrix products: 4.28 us -> none  [the longest x2 3.26 us: window_cols(): jnp.einsum('p...i,pij->p...j', lead_part, band_lead, preferred_element_ty...]
    ppermute x1, waiting for transfers between devices: 0.01 us -> 3.65 us  [extended_2(): lax.ppermute(lax.slice_in_dim(block, 0, width, axis=dim), axis, backward)]
    add x4 -> x0, other arithmetic: 3.18 us -> none  [the longest x1 3.11 us: slot_fields(): own_data[:, :, 0] * partner_data[:, :, 0]]
    gather x1 -> x0, local copies, waits for them, and re-layouts: 2.48 us -> none  [local(): extended[static_index].reshape((per_dev, MAXP) + extended.shape[1:])]
  transfers between devices with their start and end apart: 4 -> 4, of which waited for: 1 -> 2; matrix products, arithmetic and copies ran while one was open for 8% -> 0% of each run, Pallas kernels for 0% -> 0%
where the time goes in v1:
time: 42 us; the launch traced here: 41.7 us
  waiting for transfers between devices  21 us (50%)
  starting transfers between devices  9.03 us (21%)
  Pallas kernels  8.1 us (19%)
  other arithmetic  1.52 us (4%)
  local copies, waits for them, and re-layouts  1.31 us (3%)
  between operations  0.73 us (2%)
    ppermute x2, waiting for transfers between devices, passed_along(): return lax.ppermute(block, axis, route)  17.4 us
    pallas_call x1, Pallas kernels, computed(): pl.pallas_call(functools.partial(compute_kernel, acq_total), grid=(per_de...  8.1 us
    ppermute x1, starting transfers between devices, extended_2(): lax.ppermute(lax.slice_in_dim(block, block.shape[dim] - width, None, axis...  4.53 us
    ppermute x1, waiting for transfers between devices, extended_2(): lax.ppermute(lax.slice_in_dim(block, 0, width, axis=dim), axis, backward)  3.65 us
    ppermute x2, starting transfers between devices, passed_along(): return lax.ppermute(block, axis, route)  2.58 us
    ppermute x1, starting transfers between devices, extended_2(): lax.ppermute(lax.slice_in_dim(block, 0, width, axis=dim), axis, backward)  1.92 us
    concatenate x1, other arithmetic, extended_2(): block = jnp.concatenate([low, block, high], axis=dim)  1.2 us
    slice x1, local copies, waits for them, and re-layouts, extended_2(): lax.slice_in_dim(block, block.shape[dim] - width, None, axis=dim)  1.18 us
  transfers between devices with their start and end apart: 4, of which 2 were waited for; matrix products, arithmetic and copies ran while one was open for 0% of the time, Pallas kernels for 0%

profile of v1, /device:TPU:1, one launch (start us, length us, event | category | flops | bytes accessed | tf_op | source)
XLA Modules:
  0.0 41.7 jit_solution(8593479724627524807)
XLA Ops:
  0.6 0.0 copy-start.1
  0.6 0.0 copy-start.2
  0.7 1.2 %fusion = (bf16[4,2,2,2048]{3,2,1,0:T(2,128)(2,1)S(1)}, bf16[4,2,2,2048]{3,2,1,0:T(2,128)(2,1)S(1)}) fusion(bf16[4,2,8,2048]{3,2,1,0:T(8,128)(2,1)} %param.3), kind=kLoop, calls=%fused_computation.2 | loop fusion | bytes 262144 | tf_op jit(solution)/shard_map/slice | solution.py:24
  1.8 4.5 %collective-permute-start = (bf16[4,2,2,2048]{3,2,1,0:T(2,128)(2,1)S(1)}, bf16[4,2,2,2048]{3,2,1,0:T(2,128)(2,1)S(1)}, u32[]{:S(2)}, u32[]{:S(2)}) collective-permute-start(bf16[4,2,2,2048]{3,2,1,0:T(2,128)(2,1)S(1)} %get-tuple-element.2), channel_id=1, source_target_pairs={{0,1},{1,2},{2,3},{4,5},{5,6},{6,7},{8,9},{9,10},{10,11},{12,13},{... | collective-permute-start | bytes 196616 | tf_op jit(solution)/shard_map/ppermute | solution.py:23
  6.4 1.9 %collective-permute-start.1 = (bf16[4,2,2,2048]{3,2,1,0:T(2,128)(2,1)S(1)}, bf16[4,2,2,2048]{3,2,1,0:T(2,128)(2,1)S(1)}, u32[]{:S(2)}, u32[]{:S(2)}) collective-permute-start(bf16[4,2,2,2048]{3,2,1,0:T(2,128)(2,1)S(1)} %get-tuple-element.3), channel_id=1, source_target_pairs={{1,0},{2,1},{3,2},{5,4},{6,5},{7,6},{9,8},{10,9},{11,10},{13,12},{... | collective-permute-start | bytes 196616 | tf_op jit(solution)/shard_map/ppermute | solution.py:26
  8.3 0.0 collective-permute-done
  8.3 3.6 %collective-permute-done.1 = bf16[4,2,2,2048]{3,2,1,0:T(2,128)(2,1)S(1)} collective-permute-done((bf16[4,2,2,2048]{3,2,1,0:T(2,128)(2,1)S(1)}, bf16[4,2,2,2048]{3,2,1,0:T(2,128)(2,1)S(1)}, u32[]{:S(2)}, u32[]{:S(2)}) %collective-permute-start.1) | collective-permute-done | bytes 65568 | tf_op jit(solution)/shard_map/ppermute | solution.py:26
  12.0 1.2 %pad_maximum_fusion.1 = bf16[4,2,12,2048]{3,2,1,0:T(8,128)(2,1)S(1)} fusion(bf16[4,2,2,2048]{3,2,1,0:T(2,128)(2,1)S(1)} %collective-permute-done.1, bf16[4,2,8,2048]{3,2,1,0:T(8,128)(2,1)} %param.3, bf16[4,2,2,2048]{3,2,1,0:T(2,128)(2,1)S(1)} %collective-permute-done), kind=kLoop, calls=%fused_computation.1 | loop fusion | flops 1179648 | bytes 786432 | tf_op jit(solution)/shard_map/concatenate | solution.py:27
  13.2 0.0 copy-start
  13.2 1.3 %collective-permute-start.2 = (bf16[4,2,12,2048]{3,2,1,0:T(8,128)(2,1)S(1)}, bf16[4,2,12,2048]{3,2,1,0:T(8,128)(2,1)S(1)}, u32[]{:S(2)}, u32[]{:S(2)}) collective-permute-start(bf16[4,2,12,2048]{3,2,1,0:T(8,128)(2,1)S(1)} %pad_maximum_fusion.1), channel_id=1, source_target_pairs={{4,0},{8,4},{12,8},{16,12},{20,16},{24,20},{28,24},{5,1},{9,5},{13... | collective-permute-start | bytes 1179656 | tf_op jit(solution)/shard_map/ppermute | solution.py:34
  14.5 1.3 %collective-permute-start.3 = (bf16[2,2,12,2048]{3,2,1,0:T(8,128)(2,1)S(1)}, bf16[2,2,12,2048]{3,2,1,0:T(8,128)(2,1)S(1)}, u32[]{:S(2)}, u32[]{:S(2)}) collective-permute-start(bf16[2,2,12,2048]{3,2,1,0:T(8,128)(2,1)S(1)} %slice.12), channel_id=1, source_target_pairs={{8,0},{12,4},{16,8},{20,12},{24,16},{28,20},{9,1},{13,5},{17,9},{2... | collective-permute-start | bytes 589832 | tf_op jit(solution)/shard_map/ppermute | solution.py:34
  15.8 0.0 copy-done.2
  15.8 0.1 copy.5.looks
  15.9 17.4 %collective-permute-done.3 = bf16[2,2,12,2048]{3,2,1,0:T(8,128)(2,1)S(1)} collective-permute-done((bf16[2,2,12,2048]{3,2,1,0:T(8,128)(2,1)S(1)}, bf16[2,2,12,2048]{3,2,1,0:T(8,128)(2,1)S(1)}, u32[]{:S(2)}, u32[]{:S(2)}) %collective-permute-start.3) | collective-permute-done | bytes 196640 | tf_op jit(solution)/shard_map/ppermute | solution.py:34
  33.3 0.0 collective-permute-done.2
  33.3 0.0 copy-done.1
  33.3 0.3 pad_maximum_fusion.src
  33.6 0.0 copy-done
  33.6 8.1 %insar_boxes.1 = (bf16[4,6,2,8,2048]{4,3,2,1,0:T(8,128)(2,1)}, bf16[4,6,8,2048]{3,2,1,0:T(8,128)(2,1)}) custom-call(s32[4]{0:T(128)S(1)} %copy-done, s32[4,2]{1,0:T(4,128)S(1)} %copy.5.looks, bf16[10,2,12,2048]{3,2,1,0:T(8,128)(2,1)S(1)} %pad_maximum_fusion.src), custom_call_target="tpu_custom_call" | custom-call | tf_op jit(solution)/shard_map/insar_boxes/pallas_call | solution.py:166
  (1 shorter events, 0.0 us)
Async XLA Ops:
  0.6 32.7 %copy-start.1 = (bf16[4,2,8,2048]{3,2,1,0:T(8,128)(2,1)S(1)}, bf16[4,2,8,2048]{3,2,1,0:T(8,128)(2,1)}, u32[]{:S(2)}) copy-start(bf16[4,2,8,2048]{3,2,1,0:T(8,128)(2,1)} %param.3) | copy-start | bytes 786436
  0.6 15.2 %copy-start.2 = (s32[4,2]{0,1:T(2,128)S(1)}, s32[4,2]{0,1:T(2,128)}, u32[]{:S(2)}) copy-start(s32[4,2]{0,1:T(2,128)} %param.5) | copy-start | bytes 100
  1.8 6.5 %collective-permute-start = (bf16[4,2,2,2048]{3,2,1,0:T(2,128)(2,1)S(1)}, bf16[4,2,2,2048]{3,2,1,0:T(2,128)(2,1)S(1)}, u32[]{:S(2)}, u32[]{:S(2)}) collective-permute-start(bf16[4,2,2,2048]{3,2,1,0:T(2,128)(2,1)S(1)} %get-tuple-element.2), channel_id=1, source_target_pairs={{0,1},{1,2},{2,3},{4,5},{5,6},{6,7},{8,9},{9,10},{10,11},{12,13},{... | collective-permute-start | bytes 196616 | tf_op jit(solution)/shard_map/ppermute | solution.py:23
  6.4 5.6 %collective-permute-start.1 = (bf16[4,2,2,2048]{3,2,1,0:T(2,128)(2,1)S(1)}, bf16[4,2,2,2048]{3,2,1,0:T(2,128)(2,1)S(1)}, u32[]{:S(2)}, u32[]{:S(2)}) collective-permute-start(bf16[4,2,2,2048]{3,2,1,0:T(2,128)(2,1)S(1)} %get-tuple-element.3), channel_id=1, source_target_pairs={{1,0},{2,1},{3,2},{5,4},{6,5},{7,6},{9,8},{10,9},{11,10},{13,12},{... | collective-permute-start | bytes 196616 | tf_op jit(solution)/shard_map/ppermute | solution.py:26
  13.2 20.5 %copy-start = (s32[4]{0:T(128)S(1)}, s32[4]{0:T(128)}, u32[]{:S(2)}) copy-start(s32[4]{0:T(128)} %counts.1) | copy-start | bytes 52
  13.2 20.1 %collective-permute-start.2 = (bf16[4,2,12,2048]{3,2,1,0:T(8,128)(2,1)S(1)}, bf16[4,2,12,2048]{3,2,1,0:T(8,128)(2,1)S(1)}, u32[]{:S(2)}, u32[]{:S(2)}) collective-permute-start(bf16[4,2,12,2048]{3,2,1,0:T(8,128)(2,1)S(1)} %pad_maximum_fusion.1), channel_id=1, source_target_pairs={{4,0},{8,4},{12,8},{16,12},{20,16},{24,20},{28,24},{5,1},{9,5},{13... | collective-permute-start | bytes 1179656 | tf_op jit(solution)/shard_map/ppermute | solution.py:34
  14.5 18.8 %collective-permute-start.3 = (bf16[2,2,12,2048]{3,2,1,0:T(8,128)(2,1)S(1)}, bf16[2,2,12,2048]{3,2,1,0:T(8,128)(2,1)S(1)}, u32[]{:S(2)}, u32[]{:S(2)}) collective-permute-start(bf16[2,2,12,2048]{3,2,1,0:T(8,128)(2,1)S(1)} %slice.12), channel_id=1, source_target_pairs={{8,0},{12,4},{16,8},{20,12},{24,16},{28,20},{9,1},{13,5},{17,9},{2... | collective-permute-start | bytes 589832 | tf_op jit(solution)/shard_map/ppermute | solution.py:34

commit v2 on v1

--- a/solution.py
+++ b/solution.py
@@ -13,52 +13,226 @@
 BLOCK = 256
 
 epsilon = 1e-06
-
-
-def extended_2(block, sides, width):
-    for axis, dim in sides:
-        count = lax.axis_size(axis)
-        forward = [(i, i + 1) for i in range(count - 1)]
-        backward = [(target, source) for source, target in forward]
-        low = lax.ppermute(
-            lax.slice_in_dim(block, block.shape[dim] - width, None, axis=dim), axis, forward
+MESH = pl.DeviceIdType.MESH
+
+
+def gather_kernel(x, held, send_sem, recv_sem):
+    tm, line = lax.axis_index("tm"), lax.axis_index("rows")
+    tm_count, line_count = lax.axis_size("tm"), lax.axis_size("rows")
+    per_dev, _, rows = x.shape[:3]
+    total = held.shape[0]
+    far = MAXP - per_dev
+    even = lax.rem(tm, 2) == 0
+    odd = lax.rem(tm, 2) == 1
+    steps = [
+        (tm >= 1, {"tm": tm - 1}),
+        (tm >= 2, {"tm": tm - 2}),
+        (tm + 1 < tm_count, {"tm": tm + 1}),
+        (tm + 2 < tm_count, {"tm": tm + 2}),
+        (line >= 1, {"rows": line - 1}),
+        (line + 1 < line_count, {"rows": line + 1}),
+    ]
+    barrier = pltpu.get_barrier_semaphore()
+    for there, device in steps:
+
+        @pl.when(there)
+        def _():
+            pl.semaphore_signal(barrier, inc=1, device_id=device, device_id_type=MESH)
+
+    pl.semaphore_wait(barrier, sum(jnp.where(there, 1, 0) for there, _ in steps))
+
+    body = pl.ds(HR, rows)
+    forward_slot = 3 * total
+    own_slot = 3 * total + far
+
+    def copy(src, dst, send, recv, device):
+        return pltpu.make_async_remote_copy(
+            src_ref=src,
+            dst_ref=dst,
+            send_sem=send_sem.at[send],
+            recv_sem=recv_sem.at[recv],
+            device_id=device,
+            device_id_type=MESH,
         )
-        high = lax.ppermute(lax.slice_in_dim(block, 0, width, axis=dim), axis, backward)
-        block = jnp.concatenate([low, block, high], axis=dim)
-    return block
-
-
-def passed_along(block, axis, distance):
-    devices = range(lax.axis_size(axis))
-    route = [(i - distance, i) for i in devices if i - distance in devices]
-    return lax.ppermute(block, axis, route)
+
+    def near(k):
+        spot = per_dev + k
+        return copy(x.at[k], held.at[spot, :, body], spot, spot, {"tm": tm - 1})
+
+    def distant(k):
+        spot = 2 * per_dev + k
+        return copy(x.at[k], held.at[spot, :, body], spot, spot, {"tm": tm - 2})
+
+    def onward(k):
+        spot = per_dev + k
+        src = held.at[2 * per_dev + k, :, body]
+        return copy(src, held.at[spot, :, body], forward_slot + k, spot, {"tm": tm + 1})
+
+    def down(p):
+        src = held.at[p, :, pl.ds(rows, HR)]
+        slot = total + p
+        return copy(src, held.at[p, :, pl.ds(0, HR)], slot, slot, {"rows": line + 1})
+
+    def up(p):
+        src = held.at[p, :, pl.ds(HR, HR)]
+        slot = 2 * total + p
+        return copy(src, held.at[p, :, pl.ds(HR + rows, HR)], slot, slot, {"rows": line - 1})
+
+    def own_down():
+        src = x.at[:, :, pl.ds(rows - HR, HR)]
+        dst = held.at[pl.ds(0, per_dev), :, pl.ds(0, HR)]
+        return copy(src, dst, own_slot, own_slot, {"rows": line + 1})
+
+    def own_up():
+        src = x.at[:, :, pl.ds(0, HR)]
+        dst = held.at[pl.ds(0, per_dev), :, pl.ds(HR + rows, HR)]
+        return copy(src, dst, own_slot + 1, own_slot + 1, {"rows": line - 1})
+
+    def has(p):
+        return tm + p // per_dev < tm_count
+
+    def spread(p):
+        @pl.when(has(p) & (line + 1 < line_count))
+        def _():
+            down(p).start()
+
+        @pl.when(has(p) & (line >= 1))
+        def _():
+            up(p).start()
+
+    def sends_near(k):
+        return (tm >= 1) & (odd if k < far else (tm >= 0))
+
+    for k in range(far):
+
+        @pl.when(tm >= 2)
+        def _():
+            distant(k).start()
+
+    for k in range(per_dev):
+
+        @pl.when(sends_near(k))
+        def _():
+            near(k).start()
+
+    @pl.when(line + 1 < line_count)
+    def _():
+        own_down().start()
+
+    @pl.when(line >= 1)
+    def _():
+        own_up().start()
+
+    for k in range(far):
+        p = 2 * per_dev + k
+
+        @pl.when(has(p))
+        def _():
+            distant(k).wait_recv()
+
+        @pl.when(has(p) & even)
+        def _():
+            onward(k).start()
+
+        spread(p)
+
+    for k in list(range(far, per_dev)) + list(range(far)):
+        p = per_dev + k
+
+        @pl.when(has(p))
+        def _():
+            near(k).wait_recv()
+
+        spread(p)
+
+    @pl.when(line >= 1)
+    def _():
+        own_down().wait_recv()
+        own_up().wait_send()
+
+    @pl.when(line + 1 < line_count)
+    def _():
+        own_up().wait_recv()
+        own_down().wait_send()
+
+    for p in range(per_dev, total):
+
+        @pl.when(has(p) & (line + 1 < line_count))
+        def _():
+            up(p).wait_recv()
+            down(p).wait_send()
+
+        @pl.when(has(p) & (line >= 1))
+        def _():
+            down(p).wait_recv()
+            up(p).wait_send()
+
+    for k in range(far):
+
+        @pl.when(tm >= 2)
+        def _():
+            distant(k).wait_send()
+
+        @pl.when(has(2 * per_dev + k) & even)
+        def _():
+            onward(k).wait_send()
+
+    for k in range(per_dev):
+
+        @pl.when(sends_near(k))
+        def _():
+            near(k).wait_send()
+
+
+def gathered(x):
+    per_dev, parts, rows, tiles, lanes = x.shape
+    total = per_dev + MAXP
+    slots = 3 * total + MAXP
+    return pl.pallas_call(
+        gather_kernel,
+        in_specs=[pl.BlockSpec(memory_space=pl.ANY)],
+        out_specs=pl.BlockSpec(memory_space=pl.ANY),
+        out_shape=jax.ShapeDtypeStruct((total, parts, rows + 2 * HR, tiles, lanes), x.dtype),
+        scratch_shapes=[pltpu.SemaphoreType.DMA((slots,)), pltpu.SemaphoreType.DMA((slots,))],
+        compiler_params=pltpu.CompilerParams(collective_id=0, has_side_effects=True),
+        name="gather_acquisitions",
+    )(x)
 
 
 def compute_kernel(
-    acq_total, counts, looks, src, ifg, coh, planes, power, sums, wide, boxed, stage
+    acq_total, counts, looks, own_src, src, ifg, coh, planes, power, sums, wide, boxed
 ):
     acq = pl.program_id(0)
-    total, _, ext_rows, cols = src.shape
+    total, _, ext_rows, tiles, _ = src.shape
     per_dev = total - MAXP
     rows = ext_rows - 2 * HR
-    tiles = cols // LANES
-    blocks = cols // BLOCK
+    blocks = tiles * LANES // BLOCK
     fields = 3 * MAXP + 1
 
     @pl.when(acq == 0)
     def _():
-        @pl.loop(0, total)
+        line = lax.axis_index("rows")
+        edge_low, edge_high = line == 0, line == lax.axis_size("rows") - 1
+
+        def place(p, r, parts):
+            outside = edge_low if r < HR else edge_high if r >= HR + rows else None
+            if outside is not None:
+                parts = [jnp.where(outside, 0.0, part) for part in parts]
+            planes[p, 0, r] = parts[0]
+            planes[p, 1, r] = parts[1]
+            power[p, r] = parts[0] * parts[0] + parts[1] * parts[1]
+
+        @pl.loop(0, per_dev)
         def _(p):
-            for part in range(2):
-                for t in range(tiles):
-                    piece = src[p, part, :, t * LANES : (t + 1) * LANES].astype(jnp.float32)
-                    stage[part, t * 16 : t * 16 + ext_rows, :] = piece
             for r in range(ext_rows):
-                real = stage[0, pl.ds(r, tiles, stride=16), :]
-                imag = stage[1, pl.ds(r, tiles, stride=16), :]
-                planes[p, 0, r] = real
-                planes[p, 1, r] = imag
-                power[p, r] = real * real + imag * imag
+                inside = HR <= r < HR + rows
+                ref, at = (own_src, r - HR) if inside else (src, r)
+                place(p, r, [ref[p, part, at].astype(jnp.float32) for part in range(2)])
+
+        @pl.loop(per_dev, total)
+        def _(p):
+            for r in range(ext_rows):
+                place(p, r, [src[p, part, r].astype(jnp.float32) for part in range(2)])
 
         zero = jnp.zeros((wide.shape[1], LANES), wide.dtype)
         wide[0, :, :LANES] = zero
@@ -158,10 +332,11 @@
             coh[0, j, :, where] = jnp.where(live, value, 0.0).astype(coh.dtype)
 
 
-def computed(extended, partner_count, look_sizes, acq_total):
-    total, _, ext_rows, cols = extended.shape
+def computed(own, extended, partner_count, look_sizes, acq_total):
+    total, _, ext_rows, tiles, _ = extended.shape
     per_dev, rows = total - MAXP, ext_rows - 2 * HR
-    tiles, blocks = cols // LANES, cols // BLOCK
+    cols = tiles * LANES
+    blocks = cols // BLOCK
     fields = 3 * MAXP + 2
     return pl.pallas_call(
         functools.partial(compute_kernel, acq_total),
@@ -169,7 +344,8 @@
         in_specs=[
             pl.BlockSpec(memory_space=pltpu.SMEM),
             pl.BlockSpec(memory_space=pltpu.SMEM),
-            pl.BlockSpec(extended.shape, lambda a: (0, 0, 0, 0)),
+            pl.BlockSpec(own.shape, lambda a: (0, 0, 0, 0, 0)),
+            pl.BlockSpec(extended.shape, lambda a: (0, 0, 0, 0, 0)),
         ],
         out_specs=[
             pl.BlockSpec((1, MAXP, 2, rows, cols), lambda a: (a, 0, 0, 0, 0)),
@@ -185,21 +361,18 @@
             pltpu.VMEM((fields, tiles * rows, LANES), jnp.float32),
             pltpu.VMEM((blocks + 1, fields * rows, BLOCK), jnp.bfloat16),
             pltpu.VMEM((blocks, fields * rows, BLOCK), jnp.float32),
-            pltpu.VMEM((2, tiles * 16, LANES), jnp.float32),
         ],
         compiler_params=pltpu.CompilerParams(vmem_limit_bytes=48 * 1024 * 1024),
         name="insar_boxes",
-    )(partner_count, look_sizes, extended)
+    )(partner_count, look_sizes, own, extended)
 
 
 def local(slc_stack, partner_count, look_sizes):
     per_dev = slc_stack.shape[0]
-    haloed = extended_2(slc_stack, (("rows", 2),), HR)
-    nearby = passed_along(haloed, "tm", -1)
-    farther = passed_along(haloed[: MAXP - per_dev], "tm", -2)
-    extended = jnp.concatenate([haloed, nearby, farther], 0)
+    tiled = slc_stack.reshape(slc_stack.shape[:-1] + (-1, LANES))
+    extended = gathered(tiled)
     acq_total = lax.axis_size("tm") * per_dev
-    return tuple(computed(extended, partner_count, look_sizes, acq_total))
+    return tuple(computed(tiled, extended, partner_count, look_sizes, acq_total))
 
 
 def solution(mesh):

time: 42 us -> 28.6 us (0.68)
  the two profiles are of different devices: /device:TPU:1 before, /device:TPU:11 now
where the time goes in v2:
time: 28.6 us; the launch traced here: 28.4 us
  Pallas kernels  23.1 us (81%)
  local copies, waits for them, and re-layouts  4.61 us (16%)
  between operations  0.66 us (2%)
    pallas_call x1, Pallas kernels, gathered(): pl.pallas_call(gather_kernel, in_specs=[pl.BlockSpec(memory_space=pl.ANY)...  15.6 us
    pallas_call x1, Pallas kernels, computed(): pl.pallas_call(functools.partial(compute_kernel, acq_total), grid=(per_de...  7.49 us
    unnamed x8, local copies, waits for them, and re-layouts  4.61 us

profile of v2, /device:TPU:11, one launch (start us, length us, event | category | flops | bytes accessed | tf_op | source)
XLA Modules:
  0.0 28.4 jit_solution(1440163749695060356)
XLA Ops:
  0.6 0.0 copy-start.2
  0.6 0.8 %copy.5.looks = s32[4,2]{1,0:T(4,128)S(1)} copy(s32[4,2]{0,1:T(2,128)} %param.5) | data formatting | bytes 64 | tf_op args[2]
  1.4 1.7 %copy.6 = bf16[8,8,16,128]{3,2,1,0:T(8,128)(2,1)} copy(bf16[8,8,16,128]{3,1,2,0:T(8,128)(2,1)} %bitcast.7) | data formatting | bytes 524288
  3.1 15.6 %gather_acquisitions.1.src = bf16[10,2,12,16,128]{4,3,2,1,0:T(8,128)(2,1)} custom-call(bf16[4,2,8,16,128]{4,3,2,1,0:T(8,128)(2,1)} %bitcast.5), custom_call_target="tpu_custom_call" | custom-call | tf_op jit(solution)/shard_map/gather_acquisitions/pallas_call | solution.py:191
  18.8 0.0 copy-done.2
  18.8 0.0 copy-start
  18.8 1.2 %copy-done = bf16[10,2,12,16,128]{4,3,2,1,0:T(8,128)(2,1)S(1)} copy-done((bf16[10,2,12,16,128]{4,3,2,1,0:T(8,128)(2,1)S(1)}, bf16[10,2,12,16,128]{4,3,2,1,0:T(8,128)(2,1)}, u32[]{:S(2)}) %copy-start) | copy-done | bytes 983064
  20.0 0.0 copy-start.1
  20.0 0.9 %copy-done.1 = bf16[8,8,16,128]{3,2,1,0:T(8,128)(2,1)S(1)} copy-done((bf16[8,8,16,128]{3,2,1,0:T(8,128)(2,1)S(1)}, bf16[8,8,16,128]{3,2,1,0:T(8,128)(2,1)}, u32[]{:S(2)}) %copy-start.1) | copy-done | bytes 262168
  20.9 7.5 %insar_boxes.1 = (bf16[4,6,2,8,2048]{4,3,2,1,0:T(8,128)(2,1)}, bf16[4,6,8,2048]{3,2,1,0:T(8,128)(2,1)}) custom-call(s32[4]{0:T(128)S(1)} %copy-done.2, s32[4,2]{1,0:T(4,128)S(1)} %copy.5.looks, bf16[4,2,8,16,128]{4,3,2,1,0:T(8,128)(2,1)S(1)} %bitcast.6, bf16[10,2,12,16,128]{4,3,2,1,0:T(8,128)(2,1)S(1)} %copy-done), custom_call_target="tpu_custom_call" | custom-call | tf_op jit(solution)/shard_map/insar_boxes/pallas_call | solution.py:341
Async XLA Ops:
  0.6 18.1 %copy-start.2 = (s32[4]{0:T(128)S(1)}, s32[4]{0:T(128)}, u32[]{:S(2)}) copy-start(s32[4]{0:T(128)} %counts.1) | copy-start | bytes 52
  18.8 1.2 %copy-start = (bf16[10,2,12,16,128]{4,3,2,1,0:T(8,128)(2,1)S(1)}, bf16[10,2,12,16,128]{4,3,2,1,0:T(8,128)(2,1)}, u32[]{:S(2)}) copy-start(bf16[10,2,12,16,128]{4,3,2,1,0:T(8,128)(2,1)} %gather_acquisitions.1.src) | copy-start | bytes 2949124
  20.0 0.9 %copy-start.1 = (bf16[8,8,16,128]{3,2,1,0:T(8,128)(2,1)S(1)}, bf16[8,8,16,128]{3,2,1,0:T(8,128)(2,1)}, u32[]{:S(2)}) copy-start(bf16[8,8,16,128]{3,2,1,0:T(8,128)(2,1)} %copy.6) | copy-start | bytes 786436

commit v3 on v2

v3 whole, which is shorter than its diff:
```python
import functools

import jax
import jax.numpy as jnp
from jax import lax
from jax.experimental import pallas as pl
from jax.experimental.pallas import tpu as pltpu
from jax.sharding import PartitionSpec as P

MAXP = 6
HR = 2
LANES = 128
BLOCK = 256

epsilon = 1e-06
MESH = pl.DeviceIdType.MESH


def kernel(
    acq_total, counts, looks, x, ifg, coh,
    held, planes, power, sums, wide, bands, own_box, send_sem, recv_sem,
):
    tm, line = lax.axis_index("tm"), lax.axis_index("rows")
    tm_count, line_count = lax.axis_size("tm"), lax.axis_size("rows")
    per_dev, _, rows = x.shape[:3]
    total = held.shape[0]
    far = MAXP - per_dev
    even = lax.rem(tm, 2) == 0
    odd = lax.rem(tm, 2) == 1
    steps = [
        (tm >= 1, {"tm": tm - 1}),
        (tm >= 2, {"tm": tm - 2}),
        (tm + 1 < tm_count, {"tm": tm + 1}),
        (tm + 2 < tm_count, {"tm": tm + 2}),
        (line >= 1, {"rows": line - 1}),
        (line + 1 < line_count, {"rows": line + 1}),
    ]
    barrier = pltpu.get_barrier_semaphore()
    for there, device in steps:

        @pl.when(there)
        def _():
            pl.semaphore_signal(barrier, inc=1, device_id=device, device_id_type=MESH)

    pl.semaphore_wait(barrier, sum(jnp.where(there, 1, 0) for there, _ in steps))

    body = pl.ds(HR, rows)
    forward_slot = 3 * total
    own_slot = 3 * total + far

    def copy(src, dst, send, recv, device):
        return pltpu.make_async_remote_copy(
            src_ref=src,
            dst_ref=dst,
            send_sem=send_sem.at[send],
            recv_sem=recv_sem.at[recv],
            device_id=device,
            device_id_type=MESH,
        )

    def near(k):
        spot = per_dev + k
        return copy(x.at[k], held.at[spot, :, body], spot, spot, {"tm": tm - 1})

    def distant(k):
        spot = 2 * per_dev + k
        return copy(x.at[k], held.at[spot, :, body], spot, spot, {"tm": tm - 2})

    def onward(k):
        spot = per_dev + k
        src = held.at[2 * per_dev + k, :, body]
        return copy(src, held.at[spot, :, body], forward_slot + k, spot, {"tm": tm + 1})

    def down(p):
        src = held.at[p, :, pl.ds(rows, HR)]
        slot = total + p
        return copy(src, held.at[p, :, pl.ds(0, HR)], slot, slot, {"rows": line + 1})

    def up(p):
        src = held.at[p, :, pl.ds(HR, HR)]
        slot = 2 * total + p
        return copy(src, held.at[p, :, pl.ds(HR + rows, HR)], slot, slot, {"rows": line - 1})

    def own_down():
        src = x.at[:, :, pl.ds(rows - HR, HR)]
        dst = held.at[pl.ds(0, per_dev), :, pl.ds(0, HR)]
        return copy(src, dst, own_slot, own_slot, {"rows": line + 1})

    def own_up():
        src = x.at[:, :, pl.ds(0, HR)]
        dst = held.at[pl.ds(0, per_dev), :, pl.ds(HR + rows, HR)]
        return copy(src, dst, own_slot + 1, own_slot + 1, {"rows": line - 1})

    def has(p):
        return tm + p // per_dev < tm_count

    def spread(p):
        @pl.when(has(p) & (line + 1 < line_count))
        def _():
            down(p).start()

        @pl.when(has(p) & (line >= 1))
        def _():
            up(p).start()

    def sends_near(k):
        return (tm >= 1) & (odd if k < far else (tm >= 0))

    for k in range(far):

        @pl.when(tm >= 2)
        def _():
            distant(k).start()

    for k in list(range(far, per_dev)) + list(range(far)):

        @pl.when(sends_near(k))
        def _():
            near(k).start()

    @pl.when(line + 1 < line_count)
    def _():
        own_down().start()

    @pl.when(line >= 1)
    def _():
        own_up().start()

    ext_rows, tiles = held.shape[2], held.shape[3]
    blocks = tiles * LANES // BLOCK
    depth = wide.shape[1]

    def outer(a):
        return jnp.where(looks[0, a] >= HR, 1.0, 0.0).astype(jnp.float32)

    def place(p, r, get):
        parts = [get(part).astype(jnp.float32) for part in range(2)]
        outside = line == 0 if r < HR else line == line_count - 1 if r >= HR + rows else None
        if outside is not None:
            parts = [jnp.where(outside, 0.0, part) for part in parts]
        planes[p, 0, r] = parts[0]
        planes[p, 1, r] = parts[1]
        power[p, r] = parts[0] * parts[0] + parts[1] * parts[1]

    def row_window(get, field, edge_weight):
        for h in range(0, tiles, 8):
            v = get(h)
            pairs = [v[r] + v[r + 1] for r in range(1, rows + 2)]
            for r in range(rows):
                total_row = pairs[r] + v[r + 3] + (v[r] + v[r + 4]) * edge_weight
                sums[field, pl.ds(h * rows + r, 8, stride=rows), :] = total_row

    def box(a, count):
        for t in range(tiles):
            m, side = (t + 1) // 2, (t + 1) % 2
            for f in range(0, count, 2):
                pieces = [
                    sums[g, t * rows : (t + 1) * rows, :] for g in range(f, min(f + 2, count))
                ]
                piece = jnp.concatenate(pieces, 0).astype(jnp.bfloat16)
                at = slice(f * rows, f * rows + len(pieces) * rows)
                wide[m, at, side * LANES : (side + 1) * LANES] = piece
        lead = wide[0:blocks].reshape(blocks * depth, BLOCK)
        tail = wide[1 : blocks + 1].reshape(blocks * depth, BLOCK)
        result = jnp.dot(lead, bands[a, 0], preferred_element_type=jnp.float32)
        result = result + jnp.dot(tail, bands[a, 1], preferred_element_type=jnp.float32)
        return result.reshape(blocks, depth, BLOCK)

    def slot(a, p):
        weight = outer(a)

        def row(q, part, r, h):
            return planes[q, part, r, h : h + 8, :]

        def real_part(h):
            return [
                row(a, 0, r, h) * row(p, 0, r, h) + row(a, 1, r, h) * row(p, 1, r, h)
                for r in range(ext_rows)
            ]

        def imag_part(h):
            return [
                row(a, 1, r, h) * row(p, 0, r, h) - row(a, 0, r, h) * row(p, 1, r, h)
                for r in range(ext_rows)
            ]

        def partner_power(h):
            return [power[p, r, h : h + 8, :] for r in range(ext_rows)]

        row_window(real_part, 0, weight)
        row_window(imag_part, 1, weight)
        row_window(partner_power, 2, weight)
        boxed = box(a, 3)
        j = p - a - 1
        live = (j < counts[a]) & (tm * per_dev + p < acq_total)
        area = ((2 * looks[0, a] + 1) * (2 * looks[1, a] + 1)).astype(jnp.float32)
        scale = 1.0 / jnp.full((rows, BLOCK), area, jnp.float32)
        for n in range(blocks):
            own = own_box[a, n]
            real, imag, other = [boxed[n, f * rows : (f + 1) * rows, :] for f in range(3)]
            magnitude = jnp.sqrt(real * real + imag * imag)
            value = magnitude * lax.rsqrt(own * other + epsilon)
            where = slice(n * BLOCK, (n + 1) * BLOCK)
            ifg[a, j, 0, :, where] = jnp.where(live, real * scale, 0.0).astype(ifg.dtype)
            ifg[a, j, 1, :, where] = jnp.where(live, imag * scale, 0.0).astype(ifg.dtype)
            coh[a, j, :, where] = jnp.where(live, value, 0.0).astype(coh.dtype)

    def arrive(p):
        @pl.when(has(p))
        def _():
            near(p - per_dev).wait_recv()

        spread(p)

    def halo(p):
        @pl.when(has(p) & (line + 1 < line_count))
        def _():
            up(p).wait_recv()

        @pl.when(has(p) & (line >= 1))
        def _():
            down(p).wait_recv()

    zero = jnp.zeros((depth, LANES), wide.dtype)
    wide[0, :, :LANES] = zero
    wide[blocks, :, LANES:] = zero
    inner = lax.broadcasted_iota(jnp.int32, (BLOCK, BLOCK), 0)
    across = lax.broadcasted_iota(jnp.int32, (BLOCK, BLOCK), 1)

    @pl.loop(0, per_dev)
    def _(a):
        reach = looks[1, a]
        bands[a, 0] = jnp.where(jnp.abs(inner - LANES - across) <= reach, 1.0, 0.0).astype(
            jnp.bfloat16
        )
        bands[a, 1] = jnp.where(jnp.abs(inner + LANES - across) <= reach, 1.0, 0.0).astype(
            jnp.bfloat16
        )
        for r in range(rows):
            place(a, HR + r, lambda part: x[a, part, r])

    @pl.when(line >= 1)
    def _():
        own_down().wait_recv()

    @pl.when(line + 1 < line_count)
    def _():
        own_up().wait_recv()

    @pl.loop(0, per_dev)
    def _(a):
        for r in list(range(HR)) + list(range(HR + rows, ext_rows)):
            place(a, r, lambda part: held[a, part, r])
        weight = outer(a)
        row_window(lambda h: [power[a, r, h : h + 8, :] for r in range(ext_rows)], 0, weight)
        own_box[a] = box(a, 1)[:, :rows, :]

    for k in range(far):
        p = 2 * per_dev + k

        @pl.when(has(p))
        def _():
            distant(k).wait_recv()

        @pl.when(has(p) & even)
        def _():
            onward(k).start()

        spread(p)

    @pl.loop(0, per_dev - 1)
    def _(a):
        @pl.loop(a + 1, per_dev)
        def _(p):
            slot(a, p)

    order = [2 * per_dev + k for k in range(far)]
    order += [per_dev + k for k in range(far, per_dev)] + [per_dev + k for k in range(far)]

    for i, p in enumerate(order):
        halo(p)
        for r in range(ext_rows):
            place(p, r, lambda part: held[p, part, r])

        @pl.loop(max(0, p - MAXP), per_dev)
        def _(a):
            slot(a, p)

        if i + 2 < len(order) and order[i + 2] < 2 * per_dev:
            arrive(order[i + 2])

    @pl.when(line >= 1)
    def _():
        own_up().wait_send()

    @pl.when(line + 1 < line_count)
    def _():
        own_down().wait_send()

    for p in range(per_dev, total):

        @pl.when(has(p) & (line + 1 < line_count))
        def _():
            down(p).wait_send()

        @pl.when(has(p) & (line >= 1))
        def _():
            up(p).wait_send()

    for k in range(far):

        @pl.when(tm >= 2)
        def _():
            distant(k).wait_send()

        @pl.when(has(2 * per_dev + k) & even)
        def _():
            onward(k).wait_send()

    for k in range(per_dev):

        @pl.when(sends_near(k))
        def _():
            near(k).wait_send()


def computed(x, counts, looks, acq_total):
    per_dev, parts, rows, tiles, lanes = x.shape
    total, ext_rows = per_dev + MAXP, rows + 2 * HR
    cols = tiles * lanes
    blocks = cols // BLOCK
    slots = 3 * total + MAXP
    smem, vmem = [pl.BlockSpec(memory_space=space) for space in (pltpu.SMEM, pltpu.VMEM)]
    return pl.pallas_call(
        functools.partial(kernel, acq_total),
        in_specs=[smem, smem, vmem],
        out_specs=[vmem, vmem],
        out_shape=[
            jax.ShapeDtypeStruct((per_dev, MAXP, 2, rows, cols), jnp.bfloat16),
            jax.ShapeDtypeStruct((per_dev, MAXP, rows, cols), jnp.bfloat16),
        ],
        scratch_shapes=[
            pltpu.VMEM((total, parts, ext_rows, tiles, lanes), x.dtype),
            pltpu.VMEM((total, parts, ext_rows, tiles, lanes), jnp.float32),
            pltpu.VMEM((total, ext_rows, tiles, lanes), jnp.float32),
            pltpu.VMEM((3, tiles * rows, lanes), jnp.float32),
            pltpu.VMEM((blocks + 1, 4 * rows, BLOCK), jnp.bfloat16),
            pltpu.VMEM((per_dev, 2, BLOCK, BLOCK), jnp.bfloat16),
            pltpu.VMEM((per_dev, blocks, rows, BLOCK), jnp.float32),
            pltpu.SemaphoreType.DMA((slots,)),
            pltpu.SemaphoreType.DMA((slots,)),
        ],
        compiler_params=pltpu.CompilerParams(
            collective_id=0, has_side_effects=True, vmem_limit_bytes=40 * 1024 * 1024
        ),
        name="insar_boxes",
    )(counts, looks, x)


def local(slc_stack, partner_count, look_sizes):
    tiled = slc_stack.reshape(slc_stack.shape[:-1] + (-1, LANES))
    acq_total = lax.axis_size("tm") * slc_stack.shape[0]
    return tuple(computed(tiled, partner_count, look_sizes.T, acq_total))


def solution(mesh):
    return jax.shard_map(
        local,
        mesh=mesh,
        in_specs=(P("tm", None, "rows", None), P("tm"), P("tm", None)),
        out_specs=(P("tm", None, None, "rows", None), P("tm", None, "rows", None)),
        check_vma=False,
    )
```

time: 28.6 us -> 25.5 us (0.89)
  the two profiles are of different devices: /device:TPU:11 before, /device:TPU:1 now
where the time goes in v3:
time: 25.5 us; the launch traced here: 25.3 us
  Pallas kernels  20.3 us (80%)
  local copies, waits for them, and re-layouts  4.34 us (17%)
  between operations  0.65 us (3%)
    pallas_call x1, Pallas kernels, computed(): pl.pallas_call(functools.partial(kernel, acq_total), in_specs=[smem, smem...  20.3 us
    unnamed x7, local copies, waits for them, and re-layouts  4.34 us

profile of v3, /device:TPU:1, one launch (start us, length us, event | category | flops | bytes accessed | tf_op | source)
XLA Modules:
  0.0 25.3 jit_solution(17952398918893094581)
XLA Ops:
  0.6 1.0 %copy.5 = bf16[8,8,16,128]{3,2,1,0:T(8,128)(2,1)S(1)} copy(bf16[8,8,16,128]{3,1,2,0:T(8,128)(2,1)} %bitcast.8) | data formatting | bytes 524288
  1.6 0.0 copy-start
  1.6 0.7 %copy-done = s32[4,2]{0,1:T(2,128)S(1)} copy-done((s32[4,2]{0,1:T(2,128)S(1)}, s32[4,2]{0,1:T(2,128)}, u32[]{:S(2)}) %copy-start) | copy-done | bytes 56
  2.3 0.0 copy-start.1
  2.3 0.7 %copy-done.1 = s32[4]{0:T(128)S(1)} copy-done((s32[4]{0:T(128)S(1)}, s32[4]{0:T(128)}, u32[]{:S(2)}) %copy-start.1) | copy-done | bytes 40
  3.0 20.3 %insar_boxes.1 = (bf16[4,6,2,8,2048]{4,3,2,1,0:T(8,128)(2,1)S(1)}, bf16[4,6,8,2048]{3,2,1,0:T(8,128)(2,1)S(1)}) custom-call(s32[4]{0:T(128)S(1)} %copy-done.1, s32[2,4]{1,0:T(2,128)S(1)} %bitcast.7, bf16[4,2,8,16,128]{4,3,2,1,0:T(8,128)(2,1)S(1)} %bitcast.6), custom_call_target="tpu_custom_call" | custom-call | tf_op jit(solution)/shard_map/insar_boxes/pallas_call | solution.py:334
  23.3 1.1 %copy.8 = bf16[4,6,2,8,2048]{4,3,2,1,0:T(8,128)(2,1)} copy(bf16[4,6,2,8,2048]{4,3,2,1,0:T(8,128)(2,1)S(1)} %get-tuple-element.4) | data formatting | bytes 3145728
  24.5 0.9 %copy.9 = bf16[4,6,8,2048]{3,2,1,0:T(8,128)(2,1)} copy(bf16[4,6,8,2048]{3,2,1,0:T(8,128)(2,1)S(1)} %get-tuple-element.5) | data formatting | bytes 1572864
Async XLA Ops:
  1.6 0.7 %copy-start = (s32[4,2]{0,1:T(2,128)S(1)}, s32[4,2]{0,1:T(2,128)}, u32[]{:S(2)}) copy-start(s32[4,2]{0,1:T(2,128)} %param.5) | copy-start | bytes 100
  2.3 0.7 %copy-start.1 = (s32[4]{0:T(128)S(1)}, s32[4]{0:T(128)}, u32[]{:S(2)}) copy-start(s32[4]{0:T(128)} %counts.1) | copy-start | bytes 52

commit v4 on v3

--- a/solution.py
+++ b/solution.py
@@ -17,8 +17,9 @@
 
 
 def kernel(
-    acq_total, counts, looks, x, ifg, coh,
-    held, planes, power, sums, wide, bands, own_box, send_sem, recv_sem,
+    acq_total, counts_in, looks_in, x, ifg, coh,
+    held, planes, power, sums, wide, bands, own_box, counts, looks,
+    send_sem, recv_sem, table_sem,
 ):
     tm, line = lax.axis_index("tm"), lax.axis_index("rows")
     tm_count, line_count = lax.axis_size("tm"), lax.axis_size("rows")
@@ -35,6 +36,12 @@
         (line >= 1, {"rows": line - 1}),
         (line + 1 < line_count, {"rows": line + 1}),
     ]
+    tables = [
+        pltpu.make_async_copy(counts_in, counts, table_sem.at[0]),
+        pltpu.make_async_copy(looks_in, looks, table_sem.at[1]),
+    ]
+    for table in tables:
+        table.start()
     barrier = pltpu.get_barrier_semaphore()
     for there, device in steps:
 
@@ -227,6 +234,9 @@
     inner = lax.broadcasted_iota(jnp.int32, (BLOCK, BLOCK), 0)
     across = lax.broadcasted_iota(jnp.int32, (BLOCK, BLOCK), 1)
 
+    for table in tables:
+        table.wait()
+
     @pl.loop(0, per_dev)
     def _(a):
         reach = looks[1, a]
@@ -330,10 +340,10 @@
     cols = tiles * lanes
     blocks = cols // BLOCK
     slots = 3 * total + MAXP
-    smem, vmem = [pl.BlockSpec(memory_space=space) for space in (pltpu.SMEM, pltpu.VMEM)]
+    hbm, vmem = [pl.BlockSpec(memory_space=space) for space in (pl.ANY, pltpu.VMEM)]
     return pl.pallas_call(
         functools.partial(kernel, acq_total),
-        in_specs=[smem, smem, vmem],
+        in_specs=[hbm, hbm, vmem],
         out_specs=[vmem, vmem],
         out_shape=[
             jax.ShapeDtypeStruct((per_dev, MAXP, 2, rows, cols), jnp.bfloat16),
@@ -347,8 +357,11 @@
             pltpu.VMEM((blocks + 1, 4 * rows, BLOCK), jnp.bfloat16),
             pltpu.VMEM((per_dev, 2, BLOCK, BLOCK), jnp.bfloat16),
             pltpu.VMEM((per_dev, blocks, rows, BLOCK), jnp.float32),
+            pltpu.SMEM((per_dev,), jnp.int32),
+            pltpu.SMEM((2, per_dev), jnp.int32),
             pltpu.SemaphoreType.DMA((slots,)),
             pltpu.SemaphoreType.DMA((slots,)),
+            pltpu.SemaphoreType.DMA((2,)),
         ],
         compiler_params=pltpu.CompilerParams(
             collective_id=0, has_side_effects=True, vmem_limit_bytes=40 * 1024 * 1024

time: 25.5 us -> 25 us (0.980)
  Pallas kernels: 20.3 us -> 19.8 us
    pallas_call x1, Pallas kernels: 20.3 us -> 19.8 us  [computed(): pl.pallas_call(functools.partial(kernel, acq_total), in_specs=[hbm, hbm,...]
where the time goes in v4:
time: 25 us; the launch traced here: 24.8 us
  Pallas kernels  19.8 us (79%)
  local copies, waits for them, and re-layouts  4.34 us (17%)
  between operations  0.65 us (3%)
    pallas_call x1, Pallas kernels, computed(): pl.pallas_call(functools.partial(kernel, acq_total), in_specs=[hbm, hbm,...  19.8 us
    unnamed x7, local copies, waits for them, and re-layouts  4.34 us

profile of v4, /device:TPU:1, one launch (start us, length us, event | category | flops | bytes accessed | tf_op | source)
XLA Modules:
  0.0 24.8 jit_solution(17244849701343912782)
XLA Ops:
  0.6 1.0 %copy.5 = bf16[8,8,16,128]{3,2,1,0:T(8,128)(2,1)S(1)} copy(bf16[8,8,16,128]{3,1,2,0:T(8,128)(2,1)} %bitcast.8) | data formatting | bytes 524288
  1.6 0.0 copy-start
  1.6 0.7 %copy-done = s32[4,2]{0,1:T(2,128)S(1)} copy-done((s32[4,2]{0,1:T(2,128)S(1)}, s32[4,2]{0,1:T(2,128)}, u32[]{:S(2)}) %copy-start) | copy-done | bytes 56
  2.3 0.0 copy-start.1
  2.3 0.7 %copy-done.1 = s32[4]{0:T(128)S(1)} copy-done((s32[4]{0:T(128)S(1)}, s32[4]{0:T(128)}, u32[]{:S(2)}) %copy-start.1) | copy-done | bytes 40
  3.0 19.8 %insar_boxes.1 = (bf16[4,6,2,8,2048]{4,3,2,1,0:T(8,128)(2,1)S(1)}, bf16[4,6,8,2048]{3,2,1,0:T(8,128)(2,1)S(1)}) custom-call(s32[4]{0:T(128)S(1)} %copy-done.1, s32[2,4]{1,0:T(2,128)S(1)} %bitcast.7, bf16[4,2,8,16,128]{4,3,2,1,0:T(8,128)(2,1)S(1)} %bitcast.6), custom_call_target="tpu_custom_call" | custom-call | tf_op jit(solution)/shard_map/insar_boxes/pallas_call | solution.py:344
  22.8 1.1 %copy.8 = bf16[4,6,2,8,2048]{4,3,2,1,0:T(8,128)(2,1)} copy(bf16[4,6,2,8,2048]{4,3,2,1,0:T(8,128)(2,1)S(1)} %get-tuple-element.4) | data formatting | bytes 3145728
  23.9 0.9 %copy.9 = bf16[4,6,8,2048]{3,2,1,0:T(8,128)(2,1)} copy(bf16[4,6,8,2048]{3,2,1,0:T(8,128)(2,1)S(1)} %get-tuple-element.5) | data formatting | bytes 1572864
Async XLA Ops:
  1.6 0.7 %copy-start = (s32[4,2]{0,1:T(2,128)S(1)}, s32[4,2]{0,1:T(2,128)}, u32[]{:S(2)}) copy-start(s32[4,2]{0,1:T(2,128)} %param.5) | copy-start | bytes 100
  2.3 0.7 %copy-start.1 = (s32[4]{0:T(128)S(1)}, s32[4]{0:T(128)}, u32[]{:S(2)}) copy-start(s32[4]{0:T(128)} %counts_in.1) | copy-start | bytes 52

commit v5 on v4

--- a/solution.py
+++ b/solution.py
@@ -51,9 +51,15 @@
 
     pl.semaphore_wait(barrier, sum(jnp.where(there, 1, 0) for there, _ in steps))
 
-    body = pl.ds(HR, rows)
-    forward_slot = 3 * total
-    own_slot = 3 * total + far
+    near_dev, far_dev, next_dev = {"tm": tm - 1}, {"tm": tm - 2}, {"tm": tm + 1}
+    starts = [per_dev, per_dev + far, 2 * per_dev]
+    sizes = [far, per_dev - far, far]
+    sides = [(0, HR), (rows - HR, rows)]
+    mid_slot = 6
+    down_slot = mid_slot + MAXP
+    up_slot = down_slot + 3
+    own_slot = up_slot + 3
+    onward_slot = own_slot + 2
 
     def copy(src, dst, send, recv, device):
         return pltpu.make_async_remote_copy(
@@ -65,28 +71,36 @@
             device_id_type=MESH,
         )
 
-    def near(k):
-        spot = per_dev + k
-        return copy(x.at[k], held.at[spot, :, body], spot, spot, {"tm": tm - 1})
-
-    def distant(k):
-        spot = 2 * per_dev + k
-        return copy(x.at[k], held.at[spot, :, body], spot, spot, {"tm": tm - 2})
-
-    def onward(k):
-        spot = per_dev + k
-        src = held.at[2 * per_dev + k, :, body]
-        return copy(src, held.at[spot, :, body], forward_slot + k, spot, {"tm": tm + 1})
-
-    def down(p):
-        src = held.at[p, :, pl.ds(rows, HR)]
-        slot = total + p
-        return copy(src, held.at[p, :, pl.ds(0, HR)], slot, slot, {"rows": line + 1})
-
-    def up(p):
-        src = held.at[p, :, pl.ds(HR, HR)]
-        slot = 2 * total + p
-        return copy(src, held.at[p, :, pl.ds(HR + rows, HR)], slot, slot, {"rows": line - 1})
+    def span(g, low, high):
+        return held.at[pl.ds(starts[g], sizes[g]), :, pl.ds(HR + low, high - low)]
+
+    def edge(g, side, device):
+        low, high = sides[side]
+        src = x.at[pl.ds(starts[g] % per_dev, sizes[g]), :, pl.ds(low, high - low)]
+        return copy(src, span(g, low, high), 2 * g + side, 2 * g + side, device)
+
+    def middle(p, device):
+        src = x.at[p % per_dev, :, pl.ds(HR, rows - 2 * HR)]
+        dst = held.at[p, :, pl.ds(2 * HR, rows - 2 * HR)]
+        slot_at = mid_slot + p - per_dev
+        return copy(src, dst, slot_at, slot_at, device)
+
+    def onward_edge(side):
+        low, high = sides[side]
+        return copy(span(2, low, high), span(0, low, high), onward_slot + side, side, next_dev)
+
+    def onward_middle(k):
+        src = held.at[2 * per_dev + k, :, pl.ds(2 * HR, rows - 2 * HR)]
+        dst = held.at[per_dev + k, :, pl.ds(2 * HR, rows - 2 * HR)]
+        return copy(src, dst, onward_slot + 2 + k, mid_slot + k, next_dev)
+
+    def down(g):
+        src, dst = span(g, rows - HR, rows), span(g, -HR, 0)
+        return copy(src, dst, down_slot + g, down_slot + g, {"rows": line + 1})
+
+    def up(g):
+        src, dst = span(g, 0, HR), span(g, rows, rows + HR)
+        return copy(src, dst, up_slot + g, up_slot + g, {"rows": line - 1})
 
     def own_down():
         src = x.at[:, :, pl.ds(rows - HR, HR)]
@@ -98,40 +112,33 @@
         dst = held.at[pl.ds(0, per_dev), :, pl.ds(HR + rows, HR)]
         return copy(src, dst, own_slot + 1, own_slot + 1, {"rows": line - 1})
 
-    def has(p):
-        return tm + p // per_dev < tm_count
-
-    def spread(p):
-        @pl.when(has(p) & (line + 1 < line_count))
-        def _():
-            down(p).start()
-
-        @pl.when(has(p) & (line >= 1))
-        def _():
-            up(p).start()
-
-    def sends_near(k):
-        return (tm >= 1) & (odd if k < far else (tm >= 0))
-
-    for k in range(far):
-
-        @pl.when(tm >= 2)
-        def _():
-            distant(k).start()
-
-    for k in list(range(far, per_dev)) + list(range(far)):
-
-        @pl.when(sends_near(k))
-        def _():
-            near(k).start()
-
-    @pl.when(line + 1 < line_count)
+    below, above = line + 1 < line_count, line >= 1
+    has = [tm + 1 < tm_count, tm + 1 < tm_count, tm + 2 < tm_count]
+    passes = even & has[2]
+    sends = [odd, tm >= 1, tm >= 2]
+    to = [near_dev, near_dev, far_dev]
+
+    @pl.when(below)
     def _():
         own_down().start()
 
-    @pl.when(line >= 1)
+    @pl.when(above)
     def _():
         own_up().start()
+
+    for g in (2, 1, 0):
+
+        @pl.when(sends[g])
+        def _():
+            for side in range(2):
+                edge(g, side, to[g]).start()
+
+    for g in (2, 1, 0):
+
+        @pl.when(sends[g])
+        def _():
+            for k in range(sizes[g]):
+                middle(starts[g] + k, to[g]).start()
 
     ext_rows, tiles = held.shape[2], held.shape[3]
     blocks = tiles * LANES // BLOCK
@@ -212,21 +219,35 @@
             ifg[a, j, 1, :, where] = jnp.where(live, imag * scale, 0.0).astype(ifg.dtype)
             coh[a, j, :, where] = jnp.where(live, value, 0.0).astype(coh.dtype)
 
-    def arrive(p):
-        @pl.when(has(p))
-        def _():
-            near(p - per_dev).wait_recv()
-
-        spread(p)
-
-    def halo(p):
-        @pl.when(has(p) & (line + 1 < line_count))
-        def _():
-            up(p).wait_recv()
-
-        @pl.when(has(p) & (line >= 1))
-        def _():
-            down(p).wait_recv()
+    def relay(g):
+        @pl.when(has[g])
+        def _():
+            for side in range(2):
+                edge(g, side, to[g]).wait_recv()
+
+        if g == 2:
+
+            @pl.when(passes)
+            def _():
+                for side in range(2):
+                    onward_edge(side).start()
+
+        @pl.when(has[g] & below)
+        def _():
+            down(g).start()
+
+        @pl.when(has[g] & above)
+        def _():
+            up(g).start()
+
+    def halo(g):
+        @pl.when(has[g] & below)
+        def _():
+            up(g).wait_recv()
+
+        @pl.when(has[g] & above)
+        def _():
+            down(g).wait_recv()
 
     zero = jnp.zeros((depth, LANES), wide.dtype)
     wide[0, :, :LANES] = zero
@@ -249,6 +270,9 @@
         for r in range(rows):
             place(a, HR + r, lambda part: x[a, part, r])
 
+    relay(2)
+    relay(1)
+
     @pl.when(line >= 1)
     def _():
         own_down().wait_recv()
@@ -265,18 +289,17 @@
         row_window(lambda h: [power[a, r, h : h + 8, :] for r in range(ext_rows)], 0, weight)
         own_box[a] = box(a, 1)[:, :rows, :]
 
-    for k in range(far):
-        p = 2 * per_dev + k
-
-        @pl.when(has(p))
-        def _():
-            distant(k).wait_recv()
-
-        @pl.when(has(p) & even)
-        def _():
-            onward(k).start()
-
-        spread(p)
+    @pl.when(has[2])
+    def _():
+        for k in range(far):
+            middle(2 * per_dev + k, far_dev).wait_recv()
+
+    @pl.when(passes)
+    def _():
+        for k in range(far):
+            onward_middle(k).start()
+
+    relay(0)
 
     @pl.loop(0, per_dev - 1)
     def _(a):
@@ -287,8 +310,17 @@
     order = [2 * per_dev + k for k in range(far)]
     order += [per_dev + k for k in range(far, per_dev)] + [per_dev + k for k in range(far)]
 
-    for i, p in enumerate(order):
-        halo(p)
+    for p in order:
+        g = 2 if p >= starts[2] else 1 if p >= starts[1] else 0
+        if g < 2:
+
+            @pl.when(has[g])
+            def _():
+                middle(p, to[g]).wait_recv()
+
+        if p == starts[g]:
+            halo(g)
+
         for r in range(ext_rows):
             place(p, r, lambda part: held[p, part, r])
 
@@ -296,42 +328,37 @@
         def _(a):
             slot(a, p)
 
-        if i + 2 < len(order) and order[i + 2] < 2 * per_dev:
-            arrive(order[i + 2])
-
-    @pl.when(line >= 1)
+    @pl.when(above)
     def _():
         own_up().wait_send()
 
-    @pl.when(line + 1 < line_count)
+    @pl.when(below)
     def _():
         own_down().wait_send()
 
-    for p in range(per_dev, total):
-
-        @pl.when(has(p) & (line + 1 < line_count))
-        def _():
-            down(p).wait_send()
-
-        @pl.when(has(p) & (line >= 1))
-        def _():
-            up(p).wait_send()
-
-    for k in range(far):
-
-        @pl.when(tm >= 2)
-        def _():
-            distant(k).wait_send()
-
-        @pl.when(has(2 * per_dev + k) & even)
-        def _():
-            onward(k).wait_send()
-
-    for k in range(per_dev):
-
-        @pl.when(sends_near(k))
-        def _():
-            near(k).wait_send()
+    for g in range(3):
+
+        @pl.when(has[g] & below)
+        def _():
+            down(g).wait_send()
+
+        @pl.when(has[g] & above)
+        def _():
+            up(g).wait_send()
+
+        @pl.when(sends[g])
+        def _():
+            for side in range(2):
+                edge(g, side, to[g]).wait_send()
+            for k in range(sizes[g]):
+                middle(starts[g] + k, to[g]).wait_send()
+
+    @pl.when(passes)
+    def _():
+        for side in range(2):
+            onward_edge(side).wait_send()
+        for k in range(far):
+            onward_middle(k).wait_send()
 
 
 def computed(x, counts, looks, acq_total):
@@ -339,8 +366,8 @@
     total, ext_rows = per_dev + MAXP, rows + 2 * HR
     cols = tiles * lanes
     blocks = cols // BLOCK
-    slots = 3 * total + MAXP
-    hbm, vmem = [pl.BlockSpec(memory_space=space) for space in (pl.ANY, pltpu.VMEM)]
+    slots = 16 + 2 * MAXP
+    hbm, vmem = [pl.BlockSpec(memory_space=space) for space in (pltpu.HBM, pltpu.VMEM)]
     return pl.pallas_call(
         functools.partial(kernel, acq_total),
         in_specs=[hbm, hbm, vmem],

time: 25 us -> 23.1 us (0.924)
  the two profiles are of different devices: /device:TPU:1 before, /device:TPU:0 now
where the time goes in v5:
time: 23.1 us; the launch traced here: 23 us
  Pallas kernels  18 us (78%)
  local copies, waits for them, and re-layouts  4.34 us (19%)
  between operations  0.65 us (3%)
    pallas_call x1, Pallas kernels, computed(): pl.pallas_call(functools.partial(kernel, acq_total), in_specs=[hbm, hbm,...  18 us
    unnamed x7, local copies, waits for them, and re-layouts  4.34 us

profile of v5, /device:TPU:0, one launch (start us, length us, event | category | flops | bytes accessed | tf_op | source)
XLA Modules:
  0.0 23.0 jit_solution(15497735696363514250)
XLA Ops:
  0.6 1.0 %copy.5 = bf16[8,8,16,128]{3,2,1,0:T(8,128)(2,1)S(1)} copy(bf16[8,8,16,128]{3,1,2,0:T(8,128)(2,1)} %bitcast.8) | data formatting | bytes 524288
  1.6 0.0 copy-start
  1.6 0.7 %copy-done = s32[4,2]{0,1:T(2,128)S(1)} copy-done((s32[4,2]{0,1:T(2,128)S(1)}, s32[4,2]{0,1:T(2,128)}, u32[]{:S(2)}) %copy-start) | copy-done | bytes 56
  2.3 0.0 copy-start.1
  2.3 0.7 %copy-done.1 = s32[4]{0:T(128)S(1)} copy-done((s32[4]{0:T(128)S(1)}, s32[4]{0:T(128)}, u32[]{:S(2)}) %copy-start.1) | copy-done | bytes 40
  3.0 18.0 %insar_boxes.1 = (bf16[4,6,2,8,2048]{4,3,2,1,0:T(8,128)(2,1)S(1)}, bf16[4,6,8,2048]{3,2,1,0:T(8,128)(2,1)S(1)}) custom-call(s32[4]{0:T(128)S(1)} %copy-done.1, s32[2,4]{1,0:T(2,128)S(1)} %bitcast.7, bf16[4,2,8,16,128]{4,3,2,1,0:T(8,128)(2,1)S(1)} %bitcast.6), custom_call_target="tpu_custom_call" | custom-call | tf_op jit(solution)/shard_map/insar_boxes/pallas_call | solution.py:371
  20.9 1.1 %copy.8 = bf16[4,6,2,8,2048]{4,3,2,1,0:T(8,128)(2,1)} copy(bf16[4,6,2,8,2048]{4,3,2,1,0:T(8,128)(2,1)S(1)} %get-tuple-element.4) | data formatting | bytes 3145728
  22.1 0.9 %copy.9 = bf16[4,6,8,2048]{3,2,1,0:T(8,128)(2,1)} copy(bf16[4,6,8,2048]{3,2,1,0:T(8,128)(2,1)S(1)} %get-tuple-element.5) | data formatting | bytes 1572864
Async XLA Ops:
  1.6 0.7 %copy-start = (s32[4,2]{0,1:T(2,128)S(1)}, s32[4,2]{0,1:T(2,128)}, u32[]{:S(2)}) copy-start(s32[4,2]{0,1:T(2,128)} %param.5) | copy-start | bytes 100
  2.3 0.7 %copy-start.1 = (s32[4]{0:T(128)S(1)}, s32[4]{0:T(128)}, u32[]{:S(2)}) copy-start(s32[4]{0:T(128)} %counts_in.1) | copy-start | bytes 52

commit v6 on v5

--- a/solution.py
+++ b/solution.py
@@ -394,7 +394,7 @@
             collective_id=0, has_side_effects=True, vmem_limit_bytes=40 * 1024 * 1024
         ),
         name="insar_boxes",
-    )(counts, looks, x)
+    )(*[pltpu.with_memory_space_constraint(table, pltpu.HBM) for table in (counts, looks)], x)
 
 
 def local(slc_stack, partner_count, look_sizes):

time: 23.1 us -> 21.8 us (0.944)
  local copies, waits for them, and re-layouts: 4.34 us -> 3.01 us
    unnamed x7 -> x3, local copies, waits for them, and re-layouts: 4.34 us -> 3.01 us
where the time goes in v6:
time: 21.8 us; the launch traced here: 21.7 us
  Pallas kernels  18 us (83%)
  local copies, waits for them, and re-layouts  3.01 us (14%)
  between operations  0.65 us (3%)
    pallas_call x1, Pallas kernels, computed(): pl.pallas_call(functools.partial(kernel, acq_total), in_specs=[hbm, hbm,...  18 us
    unnamed x3, local copies, waits for them, and re-layouts  3.01 us

profile of v6, /device:TPU:0, one launch (start us, length us, event | category | flops | bytes accessed | tf_op | source)
XLA Modules:
  0.0 21.7 jit_solution(7661688934115273340)
XLA Ops:
  0.6 1.0 %copy.5 = bf16[8,8,16,128]{3,2,1,0:T(8,128)(2,1)S(1)} copy(bf16[8,8,16,128]{3,1,2,0:T(8,128)(2,1)} %bitcast.7) | data formatting | bytes 524288
  1.6 18.0 %insar_boxes.1 = (bf16[4,6,2,8,2048]{4,3,2,1,0:T(8,128)(2,1)S(1)}, bf16[4,6,8,2048]{3,2,1,0:T(8,128)(2,1)S(1)}) custom-call(s32[4]{0:T(128)} %counts_in.1, s32[2,4]{1,0:T(2,128)} %bitcast.8, bf16[4,2,8,16,128]{4,3,2,1,0:T(8,128)(2,1)S(1)} %bitcast.6), custom_call_target="tpu_custom_call" | custom-call | tf_op jit(solution)/shard_map/insar_boxes/pallas_call | solution.py:371
  19.7 1.1 %copy.8 = bf16[4,6,2,8,2048]{4,3,2,1,0:T(8,128)(2,1)} copy(bf16[4,6,2,8,2048]{4,3,2,1,0:T(8,128)(2,1)S(1)} %get-tuple-element.4) | data formatting | bytes 3145728
  20.8 0.9 %copy.9 = bf16[4,6,8,2048]{3,2,1,0:T(8,128)(2,1)} copy(bf16[4,6,8,2048]{3,2,1,0:T(8,128)(2,1)S(1)} %get-tuple-element.5) | data formatting | bytes 1572864
